TPU v7x, 32 devices: a whole 2x2x4 slice. The times are simulated.
32 devices in a mesh: ctx: 8 (over z, y), head: 4 (over x, core).
Axes of the slice: x: 2, y: 2, z: 4, core: 2. Of those that a mesh axis runs over, the one named last changes fastest.
Arguments:
- tokens: bfloat16 [4096, 2048], P('ctx', 'head'), may hold values from -6 to 6
- value_weight: bfloat16 [2048, 4096], P('ctx', 'head'), may hold values from -0.125 to 0.125
- queries: bfloat16 [4096, 128], P('ctx'), may hold values from -2.390625 to 2.390625
- key_vectors: bfloat16 [4096, 128], P('ctx'), may hold values from -2.390625 to 2.390625
- level_weight: float32 [13, 64, 4096], P(None, 'head', 'ctx'), may hold values from 0.2 to 1
Outputs:
- attended: bfloat16 [4096, 4096], P('ctx', 'head')
All inputs are finite; a program needn't handle non-finite values.
Results may differ from a plain program's by a relative error of at most 0.006.
Values may be sent and summed in bfloat16 or wider, within the bound.
No kernel may reach another device: no remote copies, remote signals or barrier semaphores. Data moves between devices by JAX's collectives and lax.ppermute only.
A program may use at most 64 MiB of HBM per device.

v0:
```python
import functools

import jax
import jax.numpy as jnp
from jax import lax
from jax.experimental import pallas as pl
from jax.experimental.pallas import tpu as pltpu
from jax.sharding import PartitionSpec as P


F32 = jnp.float32
BF16 = jnp.bfloat16


def from_partner(block, axis, distance, both=True):
    count = lax.axis_size(axis)
    route = []
    for low in range(count):
        high = low | 1 << distance
        if high != low and high < count:
            route += [(low, high), (high, low)] if both else [(low, high)]
    return lax.ppermute(block, axis, route)


def gather_pieces(block, axis):
    pieces = [block]
    masks = [0]
    for bit in reversed(range(lax.axis_size(axis).bit_length() - 1)):
        for mask, piece in zip(list(masks), list(pieces)):
            pieces.append(from_partner(piece, axis, bit))
            masks.append(mask | 1 << bit)
    return [piece for _, piece in sorted(zip(masks, pieces), key=lambda pair: pair[0])]


def level_scale(level_num):
    return 1.0 if level_num == 0 else 2.0 ** (-(level_num - 1) / 2.0)


def on_chip(*arrays):
    return [pltpu.with_memory_space_constraint(array, pltpu.VMEM) for array in arrays]


def off_chip(*arrays):
    return [pltpu.with_memory_space_constraint(array, pltpu.HBM) for array in arrays]


def dot_last(left, right):
    return lax.dot_general(left, right, (((1,), (1,)), ((), ())), preferred_element_type=F32)


def spread_rows(row, count):
    return jnp.broadcast_to(row, (count, row.shape[1]))


def prepare_kernel(q_hbm, k_hbm, w_hbm, near_ref, score_ref, row_ref, q_ref, k_ref, w_ref, sems):
    loads = [
        pltpu.make_async_copy(source, target, sems.at[num])
        for num, (source, target) in enumerate([(q_hbm, q_ref), (k_hbm, k_ref), (w_hbm, w_ref)])
    ]
    for load in loads:
        load.start()
    for load in loads:
        load.wait()
    length = q_ref.shape[0]
    heads, _, rows = near_ref.shape
    tile = min(128, length)
    sub = 8
    tile_levels = tile.bit_length() - 1
    sub_levels = sub.bit_length() - 1
    score_ref[...] = dot_last(k_ref[...], q_ref[...]).astype(BF16)
    for num in range(rows.bit_length()):
        for head in range(heads):
            row_ref[head, num : num + 1, :] = w_ref[num, head : head + 1, :] * level_scale(num)

    def grid_level(shape, shift):
        s_pos = lax.broadcasted_iota(jnp.int32, shape, 0)
        t_pos = jnp.right_shift(lax.broadcasted_iota(jnp.int32, shape, 1), shift)
        if shift == 0:
            t_pos = jnp.bitwise_and(t_pos, sub - 1)
        differ = jnp.bitwise_xor(s_pos, t_pos)
        level = jnp.zeros(shape, jnp.int32)
        for bit in range(tile_levels):
            level = level + (jnp.right_shift(differ, bit) > 0).astype(jnp.int32)
        return jnp.where(s_pos <= t_pos, level, -1)

    fine = grid_level((sub, tile), 0)
    coarse = grid_level((tile // sub, tile), sub_levels)
    near_diag = lax.broadcasted_iota(jnp.int32, (tile, tile), 0) // sub == (
        lax.broadcasted_iota(jnp.int32, (tile, tile), 1) // sub
    )

    def one_head(head, carry):
        for t0 in range(0, length, tile):
            base = t0 // rows * rows
            weight_rows = [
                row_ref[head, num : num + 1, t0 : t0 + tile] for num in range(rows.bit_length())
            ]
            for s0 in range(base, base + rows, tile):
                place_at = (head, pl.ds(s0, tile), pl.ds(t0 - base, tile))
                if s0 > t0:
                    near_ref[place_at] = jnp.zeros((tile, tile), BF16)
                    continue
                if s0 == t0:
                    small = jnp.zeros((sub, tile), F32)
                    for num in range(sub_levels + 1):
                        small = jnp.where(fine == num, spread_rows(weight_rows[num], sub), small)
                    big = jnp.zeros((tile // sub, tile), F32)
                    for num in range(sub_levels + 1, tile_levels + 1):
                        big = jnp.where(
                            coarse == num - sub_levels,
                            spread_rows(weight_rows[num], tile // sub),
                            big,
                        )
                    big = jnp.concatenate(
                        [spread_rows(big[row : row + 1], sub) for row in range(tile // sub)], axis=0
                    )
                    weight = jnp.where(near_diag, jnp.concatenate([small] * (tile // sub), 0), big)
                else:
                    num = tile_levels + (s0 // tile ^ t0 // tile).bit_length()
                    weight = spread_rows(weight_rows[num], tile)
                score = score_ref[s0 : s0 + tile, t0 : t0 + tile].astype(F32)
                near_ref[place_at] = (weight * score).astype(BF16)
        return carry

    lax.fori_loop(0, heads, one_head, 0)


def prepare(queries, key_vectors, level_weight):
    length = queries.shape[0]
    heads = level_weight.shape[1]
    rows = min(256, length)
    return pl.pallas_call(
        prepare_kernel,
        in_specs=[pl.BlockSpec(memory_space=pltpu.HBM)] * 3,
        out_shape=[
            pltpu.VMEM((heads, length, rows), BF16),
            pltpu.VMEM((length, length), BF16),
        ],
        scratch_shapes=[
            pltpu.VMEM((heads, rows.bit_length(), length), F32),
            pltpu.VMEM(queries.shape, queries.dtype),
            pltpu.VMEM(key_vectors.shape, key_vectors.dtype),
            pltpu.VMEM(level_weight.shape, level_weight.dtype),
            pltpu.SemaphoreType.DMA((3,)),
        ],
        compiler_params=pltpu.CompilerParams(vmem_limit_bytes=16 << 20),
        name="prepare",
    )(*off_chip(queries, key_vectors, level_weight))


def begin_kernel(k_hbm, token_hbm, weight_hbm, sum_ref, sent_ref, held_ref, *rest):
    part_refs, (k_ref, weight_ref, sems) = rest[:-3], rest[-3:]
    loads = [
        pltpu.make_async_copy(source, target, sems.at[num])
        for num, (source, target) in enumerate(
            [(k_hbm, k_ref), (token_hbm, held_ref), (weight_hbm, weight_ref)]
        )
    ]
    for load in loads:
        load.start()
    loads[0].wait()
    loads[1].wait()
    total = lax.dot_general(
        k_ref[...], held_ref[...], (((0,), (0,)), ((), ())), preferred_element_type=F32
    )
    sum_ref[...] = total
    sent_ref[...] = total.astype(BF16)
    loads[2].wait()
    share = part_refs[0].shape[0]
    for num, part_ref in enumerate(part_refs):
        part_ref[...] = weight_ref[:, num * share : (num + 1) * share].T


def begin(key_vectors, tokens, weight, split):
    depth, width = weight.shape
    shape = (key_vectors.shape[1], tokens.shape[1])
    return pl.pallas_call(
        begin_kernel,
        in_specs=[pl.BlockSpec(memory_space=pltpu.HBM)] * 3,
        out_shape=[
            pltpu.VMEM(shape, F32),
            pltpu.VMEM(shape, BF16),
            pltpu.VMEM(tokens.shape, tokens.dtype),
        ]
        + [pltpu.VMEM((width // split, depth), weight.dtype)] * split,
        scratch_shapes=[
            pltpu.VMEM(key_vectors.shape, key_vectors.dtype),
            pltpu.VMEM(weight.shape, weight.dtype),
            pltpu.SemaphoreType.DMA((3,)),
        ],
        compiler_params=pltpu.CompilerParams(vmem_limit_bytes=8 << 20),
        name="begin",
    )(*off_chip(key_vectors, tokens, weight))


def cut_kernel(count, *refs):
    for num in range(count):
        block_ref, parts = refs[num], refs[count + 2 * num :][:2]
        rows = parts[0].shape[0]
        parts[0][...] = block_ref[:rows, :]
        parts[1][...] = block_ref[rows:, :]


def cut(blocks):
    return pl.pallas_call(
        functools.partial(cut_kernel, len(blocks)),
        in_specs=[pl.BlockSpec(memory_space=pltpu.VMEM)] * len(blocks),
        out_shape=[
            pltpu.VMEM((block.shape[0] // 2, block.shape[1]), block.dtype)
            for block in blocks
            for _ in range(2)
        ],
        compiler_params=pltpu.CompilerParams(vmem_limit_bytes=4 << 20),
    )(*blocks)


def ring_order(count):
    return list(range(0, count, 2)) + list(range(1, count, 2))[::-1]


def place(offset, depth, piece_width):
    count = lax.axis_size("ctx")
    mine = lax.axis_index("ctx")
    pos = jnp.where(mine % 2 == 0, mine // 2, count - 1 - mine // 2)
    pos = (pos + offset + count) % count
    index = jnp.where(pos < count // 2, 2 * pos, 2 * (count - 1 - pos) + 1)
    per_piece = piece_width // depth
    return jnp.bitwise_xor(index // per_piece, lax.axis_index("head")), index % per_piece * depth


def choose(offsets, pieces, depth, chosen_ref):
    for num, offset in enumerate(offsets):
        piece, start = place(offset, depth, pieces[0].shape[1])
        start = pl.multiple_of(start, 128)
        for index, ref in enumerate(pieces):

            @pl.when(piece == index)
            def _():
                chosen_ref[:, num * depth : (num + 1) * depth] = ref[:, pl.ds(start, depth)]


def extend_kernel(sizes, offsets, split, started, *refs):
    refs = list(refs)
    take = lambda count: [refs.pop(0) for _ in range(count)]
    groups = [take(size) for size in sizes]
    blocks = [take(split) for _ in offsets]
    totals = take(len(sizes)) if started else []
    out_refs, chosen_refs = take(len(sizes)), refs
    share, depth = blocks[0][0].shape
    for pieces, chosen_ref in zip(groups, chosen_refs):
        choose(offsets, pieces, depth, chosen_ref)
    step = min(256, share)
    for c0 in range(0, share * split, step):
        at = c0 % share
        left = jnp.concatenate(
            [block[c0 // share][at : at + step, :] for block in blocks], axis=1
        )
        for num, (out_ref, chosen_ref) in enumerate(zip(out_refs, chosen_refs)):
            total = dot_last(left, chosen_ref[...])
            if started:
                total = total + totals[num][c0 : c0 + step, :]
            out_ref[c0 : c0 + step, :] = total


def extend(totals, groups, parts):
    offsets = tuple(offset for offset, _ in parts)
    blocks = [half for _, block in parts for half in block]
    split = len(parts[0][1])
    share, depth = blocks[0].shape
    arrays = [*(piece for pieces in groups for piece in pieces), *blocks, *totals]
    rows = [pieces[0].shape[0] for pieces in groups]
    return pl.pallas_call(
        functools.partial(
            extend_kernel, [len(pieces) for pieces in groups], offsets, split, len(totals) > 0
        ),
        in_specs=[pl.BlockSpec(memory_space=pltpu.VMEM)] * len(arrays),
        out_shape=[pltpu.VMEM((share * split, count), F32) for count in rows],
        scratch_shapes=[pltpu.VMEM((count, depth * len(parts)), BF16) for count in rows],
        compiler_params=pltpu.CompilerParams(vmem_limit_bytes=12 << 20),
    )(*arrays)


def finish_kernel(piece_count, groups, offset, last_at, carried_at, final, head_size, *refs):
    last_count = len(last_at)
    refs = list(refs)
    take = lambda count: [refs.pop(0) for _ in range(count)]
    token_refs, sum_refs = take(piece_count), [take(piece_count) for _ in range(groups)]
    last_refs = take(last_count)
    value_ref, state_refs = refs.pop(0), take(groups)
    q_ref, w_ref, near_ref, score_ref = take(4)
    carried_refs = take(len(carried_at))
    width = value_ref.shape[0]
    step = min(256, width)
    columns = [(c0, None) for c0 in range(0, width, step)]
    if last_count:
        columns = [
            (start + c0, ref.at[c0 : c0 + step, :])
            for start, ref in zip(last_at, last_refs)
            for c0 in range(0, ref.shape[0], step)
        ]
    out_refs = take(1 if final else len(columns))
    stores = []
    if final:
        held_ref, sems = refs.pop(), refs.pop()

        def store(source, start, low):
            stores.append(
                pltpu.make_async_copy(
                    source,
                    out_refs[0].at[low : low + source.shape[0], start : start + step],
                    sems.at[len(stores)],
                )
            )
            stores[-1].start()

        for start, ref in zip(carried_at, carried_refs):
            store(ref, start, 0)
    length, state_rows = q_ref.shape
    near_levels = length.bit_length()
    far_levels = w_ref.shape[0] - near_levels
    rows = near_ref.shape[2]
    if last_count:
        token_chosen, *sum_chosen = refs
        depth = token_chosen.shape[1]
        choose([offset], token_refs, depth, token_chosen)
        for pieces, chosen in zip(sum_refs, sum_chosen):
            choose([offset], pieces, depth, chosen)
    mine = lax.axis_index("ctx")
    queries = q_ref[...]
    twice = jnp.concatenate([queries, queries], axis=1)
    for num, (c0, last_ref) in enumerate(columns):
        out_ref = held_ref.at[:, c0 : c0 + step] if final else out_refs[num]
        values = value_ref[c0 : c0 + step, :]
        states = [ref[c0 : c0 + step, :] for ref in state_refs]
        if last_count:
            left = last_ref[...]
            values = values + dot_last(left, token_chosen[...])
            states = [
                part + dot_last(left, chosen[...]) for part, chosen in zip(states, sum_chosen)
            ]
        values = values.astype(BF16)
        heads = range(c0 // head_size, (c0 + step) // head_size)

        def weight(level, low, high):
            return jnp.concatenate(
                [
                    spread_rows(
                        w_ref[level, head : head + 1, low:high] * level_scale(level), head_size
                    )
                    for head in heads
                ],
                axis=0,
            )

        far = None
        states = jnp.concatenate(states, axis=1)
        for far_num in range(far_levels):
            state = states[:, far_num * state_rows : (far_num + 1) * state_rows]
            state = jnp.where(jnp.right_shift(mine, far_num) % 2 == 1, state, jnp.zeros_like(state))
            high = state.astype(BF16)
            low = (state - high.astype(F32)).astype(BF16)
            reading = dot_last(jnp.concatenate([high, low], axis=1), twice)
            reading = weight(near_levels + far_num, 0, length) * reading
            far = reading if far is None else far + reading
        for t0 in range(0, length, rows):
            total = far[:, t0 : t0 + rows] + jnp.concatenate(
                [
                    jnp.dot(
                        values[head * head_size - c0 : (head + 1) * head_size - c0, t0 : t0 + rows],
                        near_ref[head, t0 : t0 + rows, :],
                        preferred_element_type=F32,
                    )
                    for head in heads
                ],
                axis=0,
            )
            for level in range(rows.bit_length(), near_levels):
                span = 1 << level - 1
                if t0 & span:
                    s0 = t0 // span * span - span
                    mixed = jnp.dot(
                        values[:, s0 : s0 + span],
                        score_ref[s0 : s0 + span, t0 : t0 + rows],
                        preferred_element_type=F32,
                    )
                    total = total + weight(level, t0, t0 + rows) * mixed
            out_ref[t0 : t0 + rows, :] = total.astype(BF16).T
            if final:
                store(out_ref.at[t0 : t0 + rows, :], c0, t0)
    for started in stores:
        started.wait()


def finish(
    values, states, offset, last, token_pieces, sum_pieces, queries, level_weight, near, head_size, carried, final
):
    width, length = values.shape
    step = min(256, width)
    flat_sums = [piece for pieces in sum_pieces for piece in pieces]
    parts = [part for _, part in last]
    held = [array for _, array in carried]
    arrays = [*token_pieces, *flat_sums, *parts, values, *states, queries, level_weight, *near, *held]
    scratch = []
    if last:
        depth = parts[0].shape[1]
        scratch = [pltpu.VMEM((rows, depth), BF16) for rows in [length, *(s.shape[1] for s in states)]]
    starts = [start + c0 for start, part in last for c0 in range(0, part.shape[0], step)]
    if final:
        scratch += [pltpu.SemaphoreType.DMA((width // step * (length // near[0].shape[2]),)), pltpu.VMEM((length, width), BF16)]
        outs = dict(
            out_shape=jax.ShapeDtypeStruct((length, width), BF16),
            out_specs=pl.BlockSpec(memory_space=pltpu.HBM),
        )
    else:
        outs = dict(out_shape=[pltpu.VMEM((length, step), BF16)] * len(starts))
    out = pl.pallas_call(
        functools.partial(
            finish_kernel,
            len(token_pieces),
            len(states),
            offset,
            [start for start, _ in last],
            [start for start, _ in carried],
            final,
            head_size,
        ),
        in_specs=[pl.BlockSpec(memory_space=pltpu.VMEM)] * len(arrays),
        scratch_shapes=scratch,
        compiler_params=pltpu.CompilerParams(vmem_limit_bytes=24 << 20),
        name="finish",
        **outs,
    )(*arrays)
    return out if final else list(zip(starts, out))


def body(tokens, value_weight, queries, key_vectors, level_weight):
    _, width_feat = tokens.shape
    depth, width_local = value_weight.shape
    head_local = level_weight.shape[1]
    head_size = width_local // head_local
    ctx_count = lax.axis_size("ctx")
    dev_bits = ctx_count.bit_length() - 1
    near = prepare(queries, key_vectors, level_weight)

    running, sent, held, *turned = begin(key_vectors, tokens, value_weight, 2)
    level_sums = []
    for section_bit in range(dev_bits):
        if section_bit > 0:
            sent = running.astype(BF16)
        if section_bit == dev_bits - 1 and dev_bits > 1:
            break
        partner = from_partner(sent, "ctx", section_bit, section_bit < dev_bits - 2)
        level_sums.append(partner)
        running = running + partner.astype(F32)
    if dev_bits > 1:
        unit = ctx_count // 4
        for hop in range(2):
            route = [((1 + hop) * unit + num, (2 + hop) * unit + num) for num in range(unit)]
            sent = lax.ppermute(sent, "ctx", route)
            top = sent if hop == 0 else top + sent
        level_sums.append(top)
    low_sums = jnp.concatenate(level_sums[:-1] or level_sums, axis=0)
    top_sums = level_sums[-1:] if dev_bits > 1 else []

    if depth % 256 or width_feat % depth:
        features = lax.all_gather(tokens, "head", axis=1, tiled=True)
        level_sums = jnp.concatenate([low_sums, *top_sums], axis=0)
        sums = lax.all_gather(level_sums, "head", axis=1, tiled=True)
        weight = lax.all_gather(value_weight, "ctx", axis=0, tiled=True)
        values = jnp.einsum("fc,tf->ct", weight, features, preferred_element_type=F32)
        states = jnp.einsum("fc,nf->cn", weight, sums, preferred_element_type=F32)
        return finish(
            values, [states], 0, [], [], [[]], queries, level_weight, near, head_size, [], True
        )

    order = ring_order(ctx_count)
    ahead = [(order[i], order[(i + 1) % ctx_count]) for i in range(ctx_count)]
    back = [(b, a) for a, b in ahead]
    half_count = ctx_count // 2
    token_pieces = on_chip(*gather_pieces(held, "head"))
    sum_pieces = [on_chip(*gather_pieces(low_sums, "head"))]
    sum_pieces += [on_chip(*gather_pieces(sums, "head")) for sums in top_sums]
    cw = ccw = tuple(turned)
    steps = [[(0, cw)]]

    def move(part, route):
        return lax.ppermute(part, "ctx", route)

    for step in range(1, half_count):
        cw = tuple(move(part, ahead) for part in cw)
        ccw = tuple(move(part, back) for part in ccw)
        steps.append([(-step, on_chip(*cw)), (step, on_chip(*ccw))])
    share = width_local // 4
    parts = [*cut([cw[0]]), *cut([ccw[1]])]
    last = [
        [(num * share, move(parts[num], ahead)), ((2 + num) * share, move(parts[2 + num], back))]
        for num in range(2)
    ]
    values = extend([], [token_pieces], steps[0] + steps[1])
    for step in range(2, half_count - 1):
        values = extend(values, [token_pieces], steps[step])
    early = [part for parts in steps[:-1] for part in parts]
    low = extend([], sum_pieces[:1], early)
    values, low = extend([*values, *low], [token_pieces, sum_pieces[0]], steps[-1])
    top = [extend([], [pieces], early + steps[-1])[0] for pieces in sum_pieces[1:]]
    states = [low, *top]
    carried = []
    for num, parts in enumerate(last):
        starts = [start for start, _ in parts]
        done = finish(
            values,
            states,
            half_count,
            list(zip(starts, on_chip(*(part for _, part in parts)))),
            token_pieces,
            sum_pieces,
            queries,
            level_weight,
            near,
            head_size,
            carried,
            num == len(last) - 1,
        )
        carried = done
    return done


def solution(mesh):
    return jax.shard_map(
        body,
        mesh=mesh,
        in_specs=(
            P("ctx", "head"),
            P("ctx", "head"),
            P("ctx", None),
            P("ctx", None),
            P(None, "head", "ctx"),
        ),
        out_specs=P("ctx", "head"),
        check_vma=False,
    )
```

profile of v0, /device:TPU:0, one launch (start us, length us, event | category | flops | bytes accessed | tf_op | source)
XLA Modules:
  0.0 78.2 jit_solution(9088187197362662882)
XLA Ops:
  0.0 1.6 %begin.1 = (f32[128,512]{1,0:T(8,128)S(1)}, bf16[128,512]{1,0:T(8,128)(2,1)S(1)}, bf16[512,512]{1,0:T(8,128)(2,1)S(1)}, bf16[512,256]{1,0:T(8,128)(2,1)S(1)}, bf16[512,256]{1,0:T(8,128)(2,1)S(1)}) custom-call(bf16[512,128]{1,0:T(8,128)(2,1)} %k_hbm.3, bf16[512,512]{1,0:T(8,128)(2,1)} %token_hbm.1, bf16[256,1024]{1,0:T(8,128)(2,1)} %weight_hbm.1), custom_call_target="tpu_custom_call" | custom-call | tf_op jit(solution)/shard_map/begin/pallas_call | solution.py:177
  1.6 3.1 %collective-permute-start.3 = (bf16[128,512]{1,0:T(8,128)(2,1)S(1)}, bf16[128,512]{1,0:T(8,128)(2,1)S(1)}, u32[]{:S(2)}, u32[]{:S(2)}) collective-permute-start(bf16[128,512]{1,0:T(8,128)(2,1)S(1)} %get-tuple-element.21), channel_id=1, source_target_pairs={{0,4},{4,0},{8,12},{12,8},{16,20},{20,16},{24,28},{28,24},{1,5},{5... | collective-permute-start | bytes 393224 | tf_op jit(solution)/shard_map/ppermute | solution.py:22
  4.7 3.5 %collective-permute-done.3 = bf16[128,512]{1,0:T(8,128)(2,1)S(1)} collective-permute-done((bf16[128,512]{1,0:T(8,128)(2,1)S(1)}, bf16[128,512]{1,0:T(8,128)(2,1)S(1)}, u32[]{:S(2)}, u32[]{:S(2)}) %collective-permute-start.3) | collective-permute-done | bytes 131104 | tf_op jit(solution)/shard_map/ppermute | solution.py:22
  8.2 3.7 %collective-permute-start.4 = (bf16[128,512]{1,0:T(8,128)(2,1)S(1)}, bf16[128,512]{1,0:T(8,128)(2,1)S(1)}, u32[]{:S(2)}, u32[]{:S(2)}) collective-permute-start(bf16[128,512]{1,0:T(8,128)(2,1)S(1)} %fusion), channel_id=1, source_target_pairs={{0,8},{4,12},{16,24},{20,28},{1,9},{5,13},{17,25},{21,29},{2,10},{... | collective-permute-start | bytes 393224 | tf_op jit(solution)/shard_map/ppermute | solution.py:22
  11.9 1.6 %collective-permute-start.24 = (bf16[512,256]{1,0:T(8,128)(2,1)S(1)}, bf16[512,256]{1,0:T(8,128)(2,1)S(1)}, u32[]{:S(2)}, u32[]{:S(2)}) collective-permute-start(bf16[512,256]{1,0:T(8,128)(2,1)S(1)} %get-tuple-element.23.refs_4_), channel_id=1, source_target_pairs={{8,0},{16,8},{24,16},{28,24},{20,28},{12,20},{4,12},{0,4},{9,1},{1... | collective-permute-start | bytes 786440 | tf_op jit(solution)/shard_map/ppermute | solution.py:487
  13.5 0.5 collective-permute-start.13
  14.0 1.2 %collective-permute-start.21 = (bf16[512,256]{1,0:T(8,128)(2,1)S(1)}, bf16[512,256]{1,0:T(8,128)(2,1)S(1)}, u32[]{:S(2)}, u32[]{:S(2)}) collective-permute-start(bf16[512,256]{1,0:T(8,128)(2,1)S(1)} %get-tuple-element.25.refs_5_), channel_id=1, source_target_pairs={{0,8},{8,16},{16,24},{24,28},{28,20},{20,12},{12,4},{4,0},{1,9},{9... | collective-permute-start | bytes 786440 | tf_op jit(solution)/shard_map/ppermute | solution.py:487
  15.2 0.8 %collective-permute-start.17 = (bf16[512,256]{1,0:T(8,128)(2,1)S(1)}, bf16[512,256]{1,0:T(8,128)(2,1)S(1)}, u32[]{:S(2)}, u32[]{:S(2)}) collective-permute-start(bf16[512,256]{1,0:T(8,128)(2,1)S(1)} %get-tuple-element.25.refs_5_), channel_id=1, source_target_pairs={{8,0},{16,8},{24,16},{28,24},{20,28},{12,20},{4,12},{0,4},{9,1},{1... | collective-permute-start | bytes 786440 | tf_op jit(solution)/shard_map/ppermute | solution.py:487
  16.1 0.7 collective-permute-start.8
  16.8 4.4 %collective-permute-done.24.refs_8_ = bf16[512,256]{1,0:T(8,128)(2,1)S(1)} collective-permute-done((bf16[512,256]{1,0:T(8,128)(2,1)S(1)}, bf16[512,256]{1,0:T(8,128)(2,1)S(1)}, u32[]{:S(2)}, u32[]{:S(2)}) %collective-permute-start.24) | collective-permute-done | bytes 262176 | tf_op jit(solution)/shard_map/ppermute | solution.py:487
  21.1 1.5 %collective-permute-start.6 = (bf16[256,512]{1,0:T(8,128)(2,1)S(1)}, bf16[256,512]{1,0:T(8,128)(2,1)S(1)}, u32[]{:S(2)}, u32[]{:S(2)}) collective-permute-start(bf16[256,512]{1,0:T(8,128)(2,1)S(1)} %constant_dynamic-update-slice_fusion.refs_0_.refs_4_), channel_id=1, source_target_pairs={{0,2},{2,0},{1,3},{3,1},{4,6},{6,4},{5,7},{7,5},{8,10},{10,8},{9,1... | collective-permute-start | bytes 786440 | tf_op jit(solution)/shard_map/ppermute | solution.py:22
  22.6 0.7 collective-permute-start.9
  23.3 0.0 collective-permute-done.13.refs_6_
  23.3 0.1 collective-permute-start.5
  23.4 2.3 %collective-permute-done.21.refs_7_ = bf16[512,256]{1,0:T(8,128)(2,1)S(1)} collective-permute-done((bf16[512,256]{1,0:T(8,128)(2,1)S(1)}, bf16[512,256]{1,0:T(8,128)(2,1)S(1)}, u32[]{:S(2)}, u32[]{:S(2)}) %collective-permute-start.21) | collective-permute-done | bytes 262176 | tf_op jit(solution)/shard_map/ppermute | solution.py:487
  25.7 1.5 %collective-permute-start.1 = (bf16[512,512]{1,0:T(8,128)(2,1)S(1)}, bf16[512,512]{1,0:T(8,128)(2,1)S(1)}, u32[]{:S(2)}, u32[]{:S(2)}) collective-permute-start(bf16[512,512]{1,0:T(8,128)(2,1)S(1)} %get-tuple-element.20.refs_0_), channel_id=1, source_target_pairs={{0,2},{2,0},{1,3},{3,1},{4,6},{6,4},{5,7},{7,5},{8,10},{10,8},{9,1... | collective-permute-start | bytes 1572872 | tf_op jit(solution)/shard_map/ppermute | solution.py:22
  27.2 0.0 collective-permute-done.17.refs_9_
  27.2 1.4 %collective-permute-start.25 = (bf16[512,256]{1,0:T(8,128)(2,1)S(1)}, bf16[512,256]{1,0:T(8,128)(2,1)S(1)}, u32[]{:S(2)}, u32[]{:S(2)}) collective-permute-start(bf16[512,256]{1,0:T(8,128)(2,1)S(1)} %collective-permute-done.24.refs_8_), channel_id=1, source_target_pairs={{8,0},{16,8},{24,16},{28,24},{20,28},{12,20},{4,12},{0,4},{9,1},{1... | collective-permute-start | bytes 786440 | tf_op jit(solution)/shard_map/ppermute | solution.py:487
  28.6 1.9 %collective-permute-start.14 = (bf16[512,256]{1,0:T(8,128)(2,1)S(1)}, bf16[512,256]{1,0:T(8,128)(2,1)S(1)}, u32[]{:S(2)}, u32[]{:S(2)}) collective-permute-start(bf16[512,256]{1,0:T(8,128)(2,1)S(1)} %collective-permute-done.13.refs_6_), channel_id=1, source_target_pairs={{0,8},{8,16},{16,24},{24,28},{28,20},{20,12},{12,4},{4,0},{1,9},{9... | collective-permute-start | bytes 786440 | tf_op jit(solution)/shard_map/ppermute | solution.py:487
  30.6 3.7 %collective-permute-start.22 = (bf16[512,256]{1,0:T(8,128)(2,1)S(1)}, bf16[512,256]{1,0:T(8,128)(2,1)S(1)}, u32[]{:S(2)}, u32[]{:S(2)}) collective-permute-start(bf16[512,256]{1,0:T(8,128)(2,1)S(1)} %collective-permute-done.21.refs_7_), channel_id=1, source_target_pairs={{0,8},{8,16},{16,24},{24,28},{28,20},{20,12},{12,4},{4,0},{1,9},{9... | collective-permute-start | bytes 786440 | tf_op jit(solution)/shard_map/ppermute | solution.py:487
  34.3 2.7 %collective-permute-done.25.refs_6_.refs_12_ = bf16[512,256]{1,0:T(8,128)(2,1)S(1)} collective-permute-done((bf16[512,256]{1,0:T(8,128)(2,1)S(1)}, bf16[512,256]{1,0:T(8,128)(2,1)S(1)}, u32[]{:S(2)}, u32[]{:S(2)}) %collective-permute-start.25) | collective-permute-done | bytes 262176 | tf_op jit(solution)/shard_map/ppermute | solution.py:487
  37.0 0.7 collective-permute-start.18
  37.7 1.3 %collective-permute-done.14.refs_4_.refs_10_ = bf16[512,256]{1,0:T(8,128)(2,1)S(1)} collective-permute-done((bf16[512,256]{1,0:T(8,128)(2,1)S(1)}, bf16[512,256]{1,0:T(8,128)(2,1)S(1)}, u32[]{:S(2)}, u32[]{:S(2)}) %collective-permute-start.14) | collective-permute-done | bytes 262176 | tf_op jit(solution)/shard_map/ppermute | solution.py:487
  39.0 2.0 %collective-permute-start.15 = (bf16[512,256]{1,0:T(8,128)(2,1)S(1)}, bf16[512,256]{1,0:T(8,128)(2,1)S(1)}, u32[]{:S(2)}, u32[]{:S(2)}) collective-permute-start(bf16[512,256]{1,0:T(8,128)(2,1)S(1)} %collective-permute-done.14.refs_4_.refs_10_), channel_id=1, source_target_pairs={{0,8},{8,16},{16,24},{24,28},{28,20},{20,12},{12,4},{4,0},{1,9},{9... | collective-permute-start | bytes 786440 | tf_op jit(solution)/shard_map/ppermute | solution.py:487
  41.0 3.6 %collective-permute-done.22.refs_5_.refs_11_ = bf16[512,256]{1,0:T(8,128)(2,1)S(1)} collective-permute-done((bf16[512,256]{1,0:T(8,128)(2,1)S(1)}, bf16[512,256]{1,0:T(8,128)(2,1)S(1)}, u32[]{:S(2)}, u32[]{:S(2)}) %collective-permute-start.22) | collective-permute-done | bytes 262176 | tf_op jit(solution)/shard_map/ppermute | solution.py:487
  44.6 0.6 collective-permute-start.11
  45.3 0.0 collective-permute-done.1.refs_2_
  45.3 0.0 collective-permute-start.2
  45.3 0.8 %collective-permute-done.18.refs_7_.refs_13_ = bf16[512,256]{1,0:T(8,128)(2,1)S(1)} collective-permute-done((bf16[512,256]{1,0:T(8,128)(2,1)S(1)}, bf16[512,256]{1,0:T(8,128)(2,1)S(1)}, u32[]{:S(2)}, u32[]{:S(2)}) %collective-permute-start.18) | collective-permute-done | bytes 262176 | tf_op jit(solution)/shard_map/ppermute | solution.py:487
  46.1 2.7 %collective-permute-start.19 = (bf16[512,256]{1,0:T(8,128)(2,1)S(1)}, bf16[512,256]{1,0:T(8,128)(2,1)S(1)}, u32[]{:S(2)}, u32[]{:S(2)}) collective-permute-start(bf16[512,256]{1,0:T(8,128)(2,1)S(1)} %collective-permute-done.18.refs_7_.refs_13_), channel_id=1, source_target_pairs={{8,0},{16,8},{24,16},{28,24},{20,28},{12,20},{4,12},{0,4},{9,1},{1... | collective-permute-start | bytes 786440 | tf_op jit(solution)/shard_map/ppermute | solution.py:487
  48.8 0.9 %collective-permute-done.11.refs_2_.refs_10_ = bf16[128,512]{1,0:T(8,128)(2,1)S(1)} collective-permute-done((bf16[128,512]{1,0:T(8,128)(2,1)S(1)}, bf16[128,512]{1,0:T(8,128)(2,1)S(1)}, u32[]{:S(2)}, u32[]{:S(2)}) %collective-permute-start.11) | collective-permute-done | bytes 131104 | tf_op jit(solution)/shard_map/ppermute | solution.py:22
  49.7 3.1 %collective-permute-start.26 = (bf16[512,256]{1,0:T(8,128)(2,1)S(1)}, bf16[512,256]{1,0:T(8,128)(2,1)S(1)}, u32[]{:S(2)}, u32[]{:S(2)}) collective-permute-start(bf16[512,256]{1,0:T(8,128)(2,1)S(1)} %collective-permute-done.25.refs_6_.refs_12_), channel_id=1, source_target_pairs={{8,0},{16,8},{24,16},{28,24},{20,28},{12,20},{4,12},{0,4},{9,1},{1... | collective-permute-start | bytes 786440 | tf_op jit(solution)/shard_map/ppermute | solution.py:487
  52.8 3.0 %collective-permute-done.19.refs_0_.refs_11_.refs_17_ = bf16[512,256]{1,0:T(8,128)(2,1)S(1)} collective-permute-done((bf16[512,256]{1,0:T(8,128)(2,1)S(1)}, bf16[512,256]{1,0:T(8,128)(2,1)S(1)}, u32[]{:S(2)}, u32[]{:S(2)}) %collective-permute-start.19) | collective-permute-done | bytes 262176 | tf_op jit(solution)/shard_map/ppermute | solution.py:487
  55.9 2.5 %collective-permute-start.27 = (bf16[256,256]{1,0:T(8,128)(2,1)S(1)}, bf16[256,256]{1,0:T(8,128)(2,1)S(1)}, u32[]{:S(2)}, u32[]{:S(2)}) collective-permute-start(bf16[256,256]{1,0:T(8,128)(2,1)S(1)} %get-tuple-element.31), channel_id=1, source_target_pairs={{0,8},{8,16},{16,24},{24,28},{28,20},{20,12},{12,4},{4,0},{1,9},{9... | collective-permute-start | bytes 393224 | tf_op jit(solution)/shard_map/ppermute | solution.py:487
  58.4 2.4 %collective-permute-done.26.refs_10_.refs_16_ = bf16[512,256]{1,0:T(8,128)(2,1)S(1)} collective-permute-done((bf16[512,256]{1,0:T(8,128)(2,1)S(1)}, bf16[512,256]{1,0:T(8,128)(2,1)S(1)}, u32[]{:S(2)}, u32[]{:S(2)}) %collective-permute-start.26) | collective-permute-done | bytes 262176 | tf_op jit(solution)/shard_map/ppermute | solution.py:487
  60.8 2.4 %collective-permute-start.28 = (bf16[256,256]{1,0:T(8,128)(2,1)S(1)}, bf16[256,256]{1,0:T(8,128)(2,1)S(1)}, u32[]{:S(2)}, u32[]{:S(2)}) collective-permute-start(bf16[256,256]{1,0:T(8,128)(2,1)S(1)} %get-tuple-element.32), channel_id=1, source_target_pairs={{8,0},{16,8},{24,16},{28,24},{20,28},{12,20},{4,12},{0,4},{9,1},{1... | collective-permute-start | bytes 393224 | tf_op jit(solution)/shard_map/ppermute | solution.py:487
  63.2 0.1 collective-permute-start.16
  63.3 2.4 %collective-permute-start.20 = (bf16[256,256]{1,0:T(8,128)(2,1)S(1)}, bf16[256,256]{1,0:T(8,128)(2,1)S(1)}, u32[]{:S(2)}, u32[]{:S(2)}) collective-permute-start(bf16[256,256]{1,0:T(8,128)(2,1)S(1)} %get-tuple-element.26), channel_id=1, source_target_pairs={{8,0},{16,8},{24,16},{28,24},{20,28},{12,20},{4,12},{0,4},{9,1},{1... | collective-permute-start | bytes 393224 | tf_op jit(solution)/shard_map/ppermute | solution.py:487
  65.7 2.8 %prepare.1 = (bf16[16,512,256]{2,1,0:T(8,128)(2,1)S(1)}, bf16[512,512]{1,0:T(8,128)(2,1)S(1)}) custom-call(bf16[512,128]{1,0:T(8,128)(2,1)} %refs_17_.3, bf16[512,128]{1,0:T(8,128)(2,1)} %k_hbm.3, f32[13,16,512]{2,1,0:T(8,128)} %refs_18_.3), custom_call_target="tpu_custom_call" | custom-call | tf_op jit(solution)/shard_map/prepare/pallas_call | solution.py:132
  68.5 1.1 %shard_map.59.refs_13_ = f32[1024,256]{1,0:T(8,128)S(1)} custom-call(bf16[256,512]{1,0:T(8,128)(2,1)S(1)} %constant_dynamic-update-slice_fusion.refs_0_.refs_4_, bf16[256,512]{1,0:T(8,128)(2,1)S(1)} %collective-permute-done.5.refs_1_.refs_5_, bf16[256,512]{1,0:T(8,128)(2,1)S(1)} %collective-permute-done.6.refs_2_.refs_6_, ...), custom_call_target="tpu_custom_call" | custom-call | tf_op jit(solution)/shard_map/pallas_call | solution.py:272
  69.6 1.4 %shard_map.61.refs_16_ = f32[1024,128]{1,0:T(8,128)S(1)} custom-call(bf16[128,512]{1,0:T(8,128)(2,1)S(1)} %add.11.refs_0_.refs_8_, bf16[128,512]{1,0:T(8,128)(2,1)S(1)} %collective-permute-done.10.refs_1_.refs_9_, bf16[128,512]{1,0:T(8,128)(2,1)S(1)} %collective-permute-done.11.refs_2_.refs_10_, ...), custom_call_target="tpu_custom_call" | custom-call | tf_op jit(solution)/shard_map/pallas_call | solution.py:272
  71.0 1.2 %shard_map.57.refs_8_ = f32[1024,512]{1,0:T(8,128)S(1)} custom-call(bf16[512,512]{1,0:T(8,128)(2,1)S(1)} %get-tuple-element.20.refs_0_, bf16[512,512]{1,0:T(8,128)(2,1)S(1)} %collective-permute-done.refs_1_, bf16[512,512]{1,0:T(8,128)(2,1)S(1)} %collective-permute-done.1.refs_2_, bf16[512,512]{1,0:T(8,128)(2,1)S(1)} %collective-permute-done.2.refs_3_, ...), custom_call_target="tpu_custom_call" | custom-call | tf_op jit(solution)/shard_map/pallas_call | solution.py:272
  72.2 0.9 %shard_map.58.refs_12_ = f32[1024,512]{1,0:T(8,128)S(1)} custom-call(bf16[512,512]{1,0:T(8,128)(2,1)S(1)} %get-tuple-element.20.refs_0_, bf16[512,512]{1,0:T(8,128)(2,1)S(1)} %collective-permute-done.refs_1_, bf16[512,512]{1,0:T(8,128)(2,1)S(1)} %collective-permute-done.1.refs_2_, bf16[512,512]{1,0:T(8,128)(2,1)S(1)} %collective-permute-done.2.refs_3_, ...), custom_call_target="tpu_custom_call" | custom-call | tf_op jit(solution)/shard_map/pallas_call | solution.py:272
  73.1 0.0 copy-start
  73.1 0.0 copy-start.1
  73.1 1.2 %shard_map.60 = (f32[1024,512]{1,0:T(8,128)S(1)}, f32[1024,256]{1,0:T(8,128)S(1)}) custom-call(bf16[512,512]{1,0:T(8,128)(2,1)S(1)} %get-tuple-element.20.refs_0_, bf16[512,512]{1,0:T(8,128)(2,1)S(1)} %collective-permute-done.refs_1_, bf16[512,512]{1,0:T(8,128)(2,1)S(1)} %collective-permute-done.1.refs_2_, ...), custom_call_target="tpu_custom_call" | custom-call | tf_op jit(solution)/shard_map/pallas_call | solution.py:272
  74.3 1.6 %finish.2 = (bf16[512,256]{1,0:T(8,128)(2,1)S(1)}, bf16[512,256]{1,0:T(8,128)(2,1)S(1)}) custom-call(bf16[512,512]{1,0:T(8,128)(2,1)S(1)} %get-tuple-element.20.refs_0_, bf16[512,512]{1,0:T(8,128)(2,1)S(1)} %collective-permute-done.refs_1_, bf16[512,512]{1,0:T(8,128)(2,1)S(1)} %collective-permute-done.1.refs_2_, ...), custom_call_target="tpu_custom_call" | custom-call | tf_op jit(solution)/shard_map/finish/pallas_call | solution.py:416
  75.9 2.3 %finish.3 = bf16[512,1024]{1,0:T(8,128)(2,1)} custom-call(bf16[512,512]{1,0:T(8,128)(2,1)S(1)} %get-tuple-element.20.refs_0_, bf16[512,512]{1,0:T(8,128)(2,1)S(1)} %collective-permute-done.refs_1_, bf16[512,512]{1,0:T(8,128)(2,1)S(1)} %collective-permute-done.1.refs_2_, bf16[512,512]{1,0:T(8,128)(2,1)S(1)} %collective-permute-done.2.refs_3_, ...), custom_call_target="tpu_custom_call" | custom-call | tf_op jit(solution)/shard_map/finish/pallas_call | solution.py:416
  (30 shorter events, 0.2 us)
Async XLA Ops:
  1.6 6.6 %collective-permute-start.3 = (bf16[128,512]{1,0:T(8,128)(2,1)S(1)}, bf16[128,512]{1,0:T(8,128)(2,1)S(1)}, u32[]{:S(2)}, u32[]{:S(2)}) collective-permute-start(bf16[128,512]{1,0:T(8,128)(2,1)S(1)} %get-tuple-element.21), channel_id=1, source_target_pairs={{0,4},{4,0},{8,12},{12,8},{16,20},{20,16},{24,28},{28,24},{1,5},{5... | collective-permute-start | bytes 393224 | tf_op jit(solution)/shard_map/ppermute | solution.py:22
  8.2 7.8 %collective-permute-start.4 = (bf16[128,512]{1,0:T(8,128)(2,1)S(1)}, bf16[128,512]{1,0:T(8,128)(2,1)S(1)}, u32[]{:S(2)}, u32[]{:S(2)}) collective-permute-start(bf16[128,512]{1,0:T(8,128)(2,1)S(1)} %fusion), channel_id=1, source_target_pairs={{0,8},{4,12},{16,24},{20,28},{1,9},{5,13},{17,25},{21,29},{2,10},{... | collective-permute-start | bytes 393224 | tf_op jit(solution)/shard_map/ppermute | solution.py:22
  11.9 9.2 %collective-permute-start.24 = (bf16[512,256]{1,0:T(8,128)(2,1)S(1)}, bf16[512,256]{1,0:T(8,128)(2,1)S(1)}, u32[]{:S(2)}, u32[]{:S(2)}) collective-permute-start(bf16[512,256]{1,0:T(8,128)(2,1)S(1)} %get-tuple-element.23.refs_4_), channel_id=1, source_target_pairs={{8,0},{16,8},{24,16},{28,24},{20,28},{12,20},{4,12},{0,4},{9,1},{1... | collective-permute-start | bytes 786440 | tf_op jit(solution)/shard_map/ppermute | solution.py:487
  13.5 9.8 %collective-permute-start.13 = (bf16[512,256]{1,0:T(8,128)(2,1)S(1)}, bf16[512,256]{1,0:T(8,128)(2,1)S(1)}, u32[]{:S(2)}, u32[]{:S(2)}) collective-permute-start(bf16[512,256]{1,0:T(8,128)(2,1)S(1)} %get-tuple-element.23.refs_4_), channel_id=1, source_target_pairs={{0,8},{8,16},{16,24},{24,28},{28,20},{20,12},{12,4},{4,0},{1,9},{9... | collective-permute-start | bytes 786440 | tf_op jit(solution)/shard_map/ppermute | solution.py:487
  14.0 11.7 %collective-permute-start.21 = (bf16[512,256]{1,0:T(8,128)(2,1)S(1)}, bf16[512,256]{1,0:T(8,128)(2,1)S(1)}, u32[]{:S(2)}, u32[]{:S(2)}) collective-permute-start(bf16[512,256]{1,0:T(8,128)(2,1)S(1)} %get-tuple-element.25.refs_5_), channel_id=1, source_target_pairs={{0,8},{8,16},{16,24},{24,28},{28,20},{20,12},{12,4},{4,0},{1,9},{9... | collective-permute-start | bytes 786440 | tf_op jit(solution)/shard_map/ppermute | solution.py:487
  15.2 12.0 %collective-permute-start.17 = (bf16[512,256]{1,0:T(8,128)(2,1)S(1)}, bf16[512,256]{1,0:T(8,128)(2,1)S(1)}, u32[]{:S(2)}, u32[]{:S(2)}) collective-permute-start(bf16[512,256]{1,0:T(8,128)(2,1)S(1)} %get-tuple-element.25.refs_5_), channel_id=1, source_target_pairs={{8,0},{16,8},{24,16},{28,24},{20,28},{12,20},{4,12},{0,4},{9,1},{1... | collective-permute-start | bytes 786440 | tf_op jit(solution)/shard_map/ppermute | solution.py:487
  16.1 6.6 %collective-permute-start.8 = (bf16[128,512]{1,0:T(8,128)(2,1)S(1)}, bf16[128,512]{1,0:T(8,128)(2,1)S(1)}, u32[]{:S(2)}, u32[]{:S(2)}) collective-permute-start(bf16[128,512]{1,0:T(8,128)(2,1)S(1)} %add_convert_fusion), channel_id=1, source_target_pairs={{8,16},{12,20},{9,17},{13,21},{10,18},{14,22},{11,19},{15,23}} | collective-permute-start | bytes 393224 | tf_op jit(solution)/shard_map/ppermute | solution.py:459
  21.1 7.5 %collective-permute-start.6 = (bf16[256,512]{1,0:T(8,128)(2,1)S(1)}, bf16[256,512]{1,0:T(8,128)(2,1)S(1)}, u32[]{:S(2)}, u32[]{:S(2)}) collective-permute-start(bf16[256,512]{1,0:T(8,128)(2,1)S(1)} %constant_dynamic-update-slice_fusion.refs_0_.refs_4_), channel_id=1, source_target_pairs={{0,2},{2,0},{1,3},{3,1},{4,6},{6,4},{5,7},{7,5},{8,10},{10,8},{9,1... | collective-permute-start | bytes 786440 | tf_op jit(solution)/shard_map/ppermute | solution.py:22
  22.6 6.0 %collective-permute-start.9 = (bf16[128,512]{1,0:T(8,128)(2,1)S(1)}, bf16[128,512]{1,0:T(8,128)(2,1)S(1)}, u32[]{:S(2)}, u32[]{:S(2)}) collective-permute-start(bf16[128,512]{1,0:T(8,128)(2,1)S(1)} %collective-permute-done.8), channel_id=1, source_target_pairs={{16,24},{20,28},{17,25},{21,29},{18,26},{22,30},{19,27},{23,31}} | collective-permute-start | bytes 393224 | tf_op jit(solution)/shard_map/ppermute | solution.py:459
  23.3 7.3 %collective-permute-start.5 = (bf16[256,512]{1,0:T(8,128)(2,1)S(1)}, bf16[256,512]{1,0:T(8,128)(2,1)S(1)}, u32[]{:S(2)}, u32[]{:S(2)}) collective-permute-start(bf16[256,512]{1,0:T(8,128)(2,1)S(1)} %constant_dynamic-update-slice_fusion.refs_0_.refs_4_), channel_id=1, source_target_pairs={{0,1},{1,0},{2,3},{3,2},{4,5},{5,4},{6,7},{7,6},{8,9},{9,8},{10,11... | collective-permute-start | bytes 786440 | tf_op jit(solution)/shard_map/ppermute | solution.py:22
  25.7 19.6 %collective-permute-start.1 = (bf16[512,512]{1,0:T(8,128)(2,1)S(1)}, bf16[512,512]{1,0:T(8,128)(2,1)S(1)}, u32[]{:S(2)}, u32[]{:S(2)}) collective-permute-start(bf16[512,512]{1,0:T(8,128)(2,1)S(1)} %get-tuple-element.20.refs_0_), channel_id=1, source_target_pairs={{0,2},{2,0},{1,3},{3,1},{4,6},{6,4},{5,7},{7,5},{8,10},{10,8},{9,1... | collective-permute-start | bytes 1572872 | tf_op jit(solution)/shard_map/ppermute | solution.py:22
  27.2 9.8 %collective-permute-start.25 = (bf16[512,256]{1,0:T(8,128)(2,1)S(1)}, bf16[512,256]{1,0:T(8,128)(2,1)S(1)}, u32[]{:S(2)}, u32[]{:S(2)}) collective-permute-start(bf16[512,256]{1,0:T(8,128)(2,1)S(1)} %collective-permute-done.24.refs_8_), channel_id=1, source_target_pairs={{8,0},{16,8},{24,16},{28,24},{20,28},{12,20},{4,12},{0,4},{9,1},{1... | collective-permute-start | bytes 786440 | tf_op jit(solution)/shard_map/ppermute | solution.py:487
  28.6 17.5 %collective-permute-start = (bf16[512,512]{1,0:T(8,128)(2,1)S(1)}, bf16[512,512]{1,0:T(8,128)(2,1)S(1)}, u32[]{:S(2)}, u32[]{:S(2)}) collective-permute-start(bf16[512,512]{1,0:T(8,128)(2,1)S(1)} %get-tuple-element.20.refs_0_), channel_id=1, source_target_pairs={{0,1},{1,0},{2,3},{3,2},{4,5},{5,4},{6,7},{7,6},{8,9},{9,8},{10,11... | collective-permute-start | bytes 1572872 | tf_op jit(solution)/shard_map/ppermute | solution.py:22
  28.6 10.4 %collective-permute-start.14 = (bf16[512,256]{1,0:T(8,128)(2,1)S(1)}, bf16[512,256]{1,0:T(8,128)(2,1)S(1)}, u32[]{:S(2)}, u32[]{:S(2)}) collective-permute-start(bf16[512,256]{1,0:T(8,128)(2,1)S(1)} %collective-permute-done.13.refs_6_), channel_id=1, source_target_pairs={{0,8},{8,16},{16,24},{24,28},{28,20},{20,12},{12,4},{4,0},{1,9},{9... | collective-permute-start | bytes 786440 | tf_op jit(solution)/shard_map/ppermute | solution.py:487
  30.6 14.1 %collective-permute-start.22 = (bf16[512,256]{1,0:T(8,128)(2,1)S(1)}, bf16[512,256]{1,0:T(8,128)(2,1)S(1)}, u32[]{:S(2)}, u32[]{:S(2)}) collective-permute-start(bf16[512,256]{1,0:T(8,128)(2,1)S(1)} %collective-permute-done.21.refs_7_), channel_id=1, source_target_pairs={{0,8},{8,16},{16,24},{24,28},{28,20},{20,12},{12,4},{4,0},{1,9},{9... | collective-permute-start | bytes 786440 | tf_op jit(solution)/shard_map/ppermute | solution.py:487
  37.0 9.1 %collective-permute-start.18 = (bf16[512,256]{1,0:T(8,128)(2,1)S(1)}, bf16[512,256]{1,0:T(8,128)(2,1)S(1)}, u32[]{:S(2)}, u32[]{:S(2)}) collective-permute-start(bf16[512,256]{1,0:T(8,128)(2,1)S(1)} %collective-permute-done.17.refs_9_), channel_id=1, source_target_pairs={{8,0},{16,8},{24,16},{28,24},{20,28},{12,20},{4,12},{0,4},{9,1},{1... | collective-permute-start | bytes 786440 | tf_op jit(solution)/shard_map/ppermute | solution.py:487
  39.0 13.8 %collective-permute-start.15 = (bf16[512,256]{1,0:T(8,128)(2,1)S(1)}, bf16[512,256]{1,0:T(8,128)(2,1)S(1)}, u32[]{:S(2)}, u32[]{:S(2)}) collective-permute-start(bf16[512,256]{1,0:T(8,128)(2,1)S(1)} %collective-permute-done.14.refs_4_.refs_10_), channel_id=1, source_target_pairs={{0,8},{8,16},{16,24},{24,28},{28,20},{20,12},{12,4},{4,0},{1,9},{9... | collective-permute-start | bytes 786440 | tf_op jit(solution)/shard_map/ppermute | solution.py:487
  44.6 5.0 %collective-permute-start.11 = (bf16[128,512]{1,0:T(8,128)(2,1)S(1)}, bf16[128,512]{1,0:T(8,128)(2,1)S(1)}, u32[]{:S(2)}, u32[]{:S(2)}) collective-permute-start(bf16[128,512]{1,0:T(8,128)(2,1)S(1)} %add.11.refs_0_.refs_8_), channel_id=1, source_target_pairs={{0,2},{2,0},{1,3},{3,1},{4,6},{6,4},{5,7},{7,5},{8,10},{10,8},{9,1... | collective-permute-start | bytes 393224 | tf_op jit(solution)/shard_map/ppermute | solution.py:22
  45.3 25.7 %collective-permute-start.2 = (bf16[512,512]{1,0:T(8,128)(2,1)S(1)}, bf16[512,512]{1,0:T(8,128)(2,1)S(1)}, u32[]{:S(2)}, u32[]{:S(2)}) collective-permute-start(bf16[512,512]{1,0:T(8,128)(2,1)S(1)} %collective-permute-done.1.refs_2_), channel_id=1, source_target_pairs={{0,1},{1,0},{2,3},{3,2},{4,5},{5,4},{6,7},{7,6},{8,9},{9,8},{10,11... | collective-permute-start | bytes 1572872 | tf_op jit(solution)/shard_map/ppermute | solution.py:22
  46.1 3.6 %collective-permute-start.10 = (bf16[128,512]{1,0:T(8,128)(2,1)S(1)}, bf16[128,512]{1,0:T(8,128)(2,1)S(1)}, u32[]{:S(2)}, u32[]{:S(2)}) collective-permute-start(bf16[128,512]{1,0:T(8,128)(2,1)S(1)} %add.11.refs_0_.refs_8_), channel_id=1, source_target_pairs={{0,1},{1,0},{2,3},{3,2},{4,5},{5,4},{6,7},{7,6},{8,9},{9,8},{10,11... | collective-permute-start | bytes 393224 | tf_op jit(solution)/shard_map/ppermute | solution.py:22
  46.1 9.7 %collective-permute-start.19 = (bf16[512,256]{1,0:T(8,128)(2,1)S(1)}, bf16[512,256]{1,0:T(8,128)(2,1)S(1)}, u32[]{:S(2)}, u32[]{:S(2)}) collective-permute-start(bf16[512,256]{1,0:T(8,128)(2,1)S(1)} %collective-permute-done.18.refs_7_.refs_13_), channel_id=1, source_target_pairs={{8,0},{16,8},{24,16},{28,24},{20,28},{12,20},{4,12},{0,4},{9,1},{1... | collective-permute-start | bytes 786440 | tf_op jit(solution)/shard_map/ppermute | solution.py:487
  49.7 6.2 %collective-permute-start.7 = (bf16[256,512]{1,0:T(8,128)(2,1)S(1)}, bf16[256,512]{1,0:T(8,128)(2,1)S(1)}, u32[]{:S(2)}, u32[]{:S(2)}) collective-permute-start(bf16[256,512]{1,0:T(8,128)(2,1)S(1)} %collective-permute-done.6.refs_2_.refs_6_), channel_id=1, source_target_pairs={{0,1},{1,0},{2,3},{3,2},{4,5},{5,4},{6,7},{7,6},{8,9},{9,8},{10,11... | collective-permute-start | bytes 786440 | tf_op jit(solution)/shard_map/ppermute | solution.py:22
  49.7 11.1 %collective-permute-start.26 = (bf16[512,256]{1,0:T(8,128)(2,1)S(1)}, bf16[512,256]{1,0:T(8,128)(2,1)S(1)}, u32[]{:S(2)}, u32[]{:S(2)}) collective-permute-start(bf16[512,256]{1,0:T(8,128)(2,1)S(1)} %collective-permute-done.25.refs_6_.refs_12_), channel_id=1, source_target_pairs={{8,0},{16,8},{24,16},{28,24},{20,28},{12,20},{4,12},{0,4},{9,1},{1... | collective-permute-start | bytes 786440 | tf_op jit(solution)/shard_map/ppermute | solution.py:487
  52.8 10.3 %collective-permute-start.23 = (bf16[512,256]{1,0:T(8,128)(2,1)S(1)}, bf16[512,256]{1,0:T(8,128)(2,1)S(1)}, u32[]{:S(2)}, u32[]{:S(2)}) collective-permute-start(bf16[512,256]{1,0:T(8,128)(2,1)S(1)} %collective-permute-done.22.refs_5_.refs_11_), channel_id=1, source_target_pairs={{0,8},{8,16},{16,24},{24,28},{28,20},{20,12},{12,4},{4,0},{1,9},{9... | collective-permute-start | bytes 786440 | tf_op jit(solution)/shard_map/ppermute | solution.py:487
  55.8 7.5 %collective-permute-start.12 = (bf16[128,512]{1,0:T(8,128)(2,1)S(1)}, bf16[128,512]{1,0:T(8,128)(2,1)S(1)}, u32[]{:S(2)}, u32[]{:S(2)}) collective-permute-start(bf16[128,512]{1,0:T(8,128)(2,1)S(1)} %collective-permute-done.11.refs_2_.refs_10_), channel_id=1, source_target_pairs={{0,1},{1,0},{2,3},{3,2},{4,5},{5,4},{6,7},{7,6},{8,9},{9,8},{10,11... | collective-permute-start | bytes 393224 | tf_op jit(solution)/shard_map/ppermute | solution.py:22
  55.9 18.4 %collective-permute-start.27 = (bf16[256,256]{1,0:T(8,128)(2,1)S(1)}, bf16[256,256]{1,0:T(8,128)(2,1)S(1)}, u32[]{:S(2)}, u32[]{:S(2)}) collective-permute-start(bf16[256,256]{1,0:T(8,128)(2,1)S(1)} %get-tuple-element.31), channel_id=1, source_target_pairs={{0,8},{8,16},{16,24},{24,28},{28,20},{20,12},{12,4},{4,0},{1,9},{9... | collective-permute-start | bytes 393224 | tf_op jit(solution)/shard_map/ppermute | solution.py:487
  60.8 13.5 %collective-permute-start.28 = (bf16[256,256]{1,0:T(8,128)(2,1)S(1)}, bf16[256,256]{1,0:T(8,128)(2,1)S(1)}, u32[]{:S(2)}, u32[]{:S(2)}) collective-permute-start(bf16[256,256]{1,0:T(8,128)(2,1)S(1)} %get-tuple-element.32), channel_id=1, source_target_pairs={{8,0},{16,8},{24,16},{28,24},{20,28},{12,20},{4,12},{0,4},{9,1},{1... | collective-permute-start | bytes 393224 | tf_op jit(solution)/shard_map/ppermute | solution.py:487
  63.2 12.7 %collective-permute-start.16 = (bf16[256,256]{1,0:T(8,128)(2,1)S(1)}, bf16[256,256]{1,0:T(8,128)(2,1)S(1)}, u32[]{:S(2)}, u32[]{:S(2)}) collective-permute-start(bf16[256,256]{1,0:T(8,128)(2,1)S(1)} %get-tuple-element.24), channel_id=1, source_target_pairs={{0,8},{8,16},{16,24},{24,28},{28,20},{20,12},{12,4},{4,0},{1,9},{9... | collective-permute-start | bytes 393224 | tf_op jit(solution)/shard_map/ppermute | solution.py:487
  63.3 12.6 %collective-permute-start.20 = (bf16[256,256]{1,0:T(8,128)(2,1)S(1)}, bf16[256,256]{1,0:T(8,128)(2,1)S(1)}, u32[]{:S(2)}, u32[]{:S(2)}) collective-permute-start(bf16[256,256]{1,0:T(8,128)(2,1)S(1)} %get-tuple-element.26), channel_id=1, source_target_pairs={{8,0},{16,8},{24,16},{28,24},{20,28},{12,20},{4,12},{0,4},{9,1},{1... | collective-permute-start | bytes 393224 | tf_op jit(solution)/shard_map/ppermute | solution.py:487
  73.1 1.2 %copy-start = (f32[13,16,512]{2,1,0:T(8,128)S(1)}, f32[13,16,512]{2,1,0:T(8,128)}, u32[]{:S(2)}) copy-start(f32[13,16,512]{2,1,0:T(8,128)} %refs_18_.3) | copy-start | bytes 1277956
  73.1 1.2 %copy-start.1 = (bf16[512,128]{1,0:T(8,128)(2,1)S(1)}, bf16[512,128]{1,0:T(8,128)(2,1)}, u32[]{:S(2)}) copy-start(bf16[512,128]{1,0:T(8,128)(2,1)} %refs_17_.3) | copy-start | bytes 393220
where the time goes:
time: 78.8 us; the launch traced here: 78.2 us
  starting transfers between devices  38.9 us (49%)
  waiting for transfers between devices  24.9 us (32%)
  Pallas kernels  14 us (18%)
    ppermute x16, starting transfers between devices, move(): return lax.ppermute(part, 'ctx', route)  27.1 us
    ppermute x16, waiting for transfers between devices, move(): return lax.ppermute(part, 'ctx', route)  20.5 us
    ppermute x11, starting transfers between devices, from_partner(): return lax.ppermute(block, axis, route)  10.5 us
    pallas_call x5, Pallas kernels, extend(): pl.pallas_call(functools.partial(extend_kernel, [len(pieces) for pieces i...  5.7 us
    ppermute x11, waiting for transfers between devices, from_partner(): return lax.ppermute(block, axis, route)  4.4 us
    pallas_call x2, Pallas kernels, finish(): pl.pallas_call(functools.partial(finish_kernel, len(token_pieces), len(st...  3.9 us
    pallas_call x1, Pallas kernels, prepare(): pl.pallas_call(prepare_kernel, in_specs=[pl.BlockSpec(memory_space=pltpu....  2.79 us
    pallas_call x1, Pallas kernels, begin(): pl.pallas_call(begin_kernel, in_specs=[pl.BlockSpec(memory_space=pltpu.HB...  1.59 us
  transfers between devices with their start and end apart: 29, of which 10 were waited for; matrix products, arithmetic and copies ran while one was open for 0% of the time, Pallas kernels for 13%

commit v1 on v0

--- a/solution.py
+++ b/solution.py
@@ -12,13 +12,13 @@
 BF16 = jnp.bfloat16
 
 
-def from_partner(block, axis, distance, both=True):
+def from_partner(block, axis, distance):
     count = lax.axis_size(axis)
     route = []
     for low in range(count):
         high = low | 1 << distance
         if high != low and high < count:
-            route += [(low, high), (high, low)] if both else [(low, high)]
+            route += [(low, high), (high, low)]
     return lax.ppermute(block, axis, route)
 
 
@@ -303,18 +303,16 @@
     if final:
         held_ref, sems = refs.pop(), refs.pop()
 
-        def store(source, start, low):
+        def store(source, start):
             stores.append(
                 pltpu.make_async_copy(
-                    source,
-                    out_refs[0].at[low : low + source.shape[0], start : start + step],
-                    sems.at[len(stores)],
+                    source, out_refs[0].at[:, start : start + step], sems.at[len(stores)]
                 )
             )
             stores[-1].start()
 
         for start, ref in zip(carried_at, carried_refs):
-            store(ref, start, 0)
+            store(ref, start)
     length, state_rows = q_ref.shape
     near_levels = length.bit_length()
     far_levels = w_ref.shape[0] - near_levels
@@ -385,8 +383,8 @@
                     )
                     total = total + weight(level, t0, t0 + rows) * mixed
             out_ref[t0 : t0 + rows, :] = total.astype(BF16).T
-            if final:
-                store(out_ref.at[t0 : t0 + rows, :], c0, t0)
+        if final:
+            store(out_ref, c0)
     for started in stores:
         started.wait()
 
@@ -406,7 +404,7 @@
         scratch = [pltpu.VMEM((rows, depth), BF16) for rows in [length, *(s.shape[1] for s in states)]]
     starts = [start + c0 for start, part in last for c0 in range(0, part.shape[0], step)]
     if final:
-        scratch += [pltpu.SemaphoreType.DMA((width // step * (length // near[0].shape[2]),)), pltpu.VMEM((length, width), BF16)]
+        scratch += [pltpu.SemaphoreType.DMA((max(1, width // step),)), pltpu.VMEM((length, width), BF16)]
         outs = dict(
             out_shape=jax.ShapeDtypeStruct((length, width), BF16),
             out_specs=pl.BlockSpec(memory_space=pltpu.HBM),
@@ -447,24 +445,13 @@
     for section_bit in range(dev_bits):
         if section_bit > 0:
             sent = running.astype(BF16)
-        if section_bit == dev_bits - 1 and dev_bits > 1:
-            break
-        partner = from_partner(sent, "ctx", section_bit, section_bit < dev_bits - 2)
+        partner = from_partner(sent, "ctx", section_bit)
         level_sums.append(partner)
         running = running + partner.astype(F32)
-    if dev_bits > 1:
-        unit = ctx_count // 4
-        for hop in range(2):
-            route = [((1 + hop) * unit + num, (2 + hop) * unit + num) for num in range(unit)]
-            sent = lax.ppermute(sent, "ctx", route)
-            top = sent if hop == 0 else top + sent
-        level_sums.append(top)
-    low_sums = jnp.concatenate(level_sums[:-1] or level_sums, axis=0)
-    top_sums = level_sums[-1:] if dev_bits > 1 else []
+    level_sums = jnp.concatenate(level_sums, axis=0)
 
     if depth % 256 or width_feat % depth:
         features = lax.all_gather(tokens, "head", axis=1, tiled=True)
-        level_sums = jnp.concatenate([low_sums, *top_sums], axis=0)
         sums = lax.all_gather(level_sums, "head", axis=1, tiled=True)
         weight = lax.all_gather(value_weight, "ctx", axis=0, tiled=True)
         values = jnp.einsum("fc,tf->ct", weight, features, preferred_element_type=F32)
@@ -478,8 +465,7 @@
     back = [(b, a) for a, b in ahead]
     half_count = ctx_count // 2
     token_pieces = on_chip(*gather_pieces(held, "head"))
-    sum_pieces = [on_chip(*gather_pieces(low_sums, "head"))]
-    sum_pieces += [on_chip(*gather_pieces(sums, "head")) for sums in top_sums]
+    sum_pieces = on_chip(*gather_pieces(level_sums, "head"))
     cw = ccw = tuple(turned)
     steps = [[(0, cw)]]
 
@@ -500,20 +486,18 @@
     for step in range(2, half_count - 1):
         values = extend(values, [token_pieces], steps[step])
     early = [part for parts in steps[:-1] for part in parts]
-    low = extend([], sum_pieces[:1], early)
-    values, low = extend([*values, *low], [token_pieces, sum_pieces[0]], steps[-1])
-    top = [extend([], [pieces], early + steps[-1])[0] for pieces in sum_pieces[1:]]
-    states = [low, *top]
+    low = extend([], [sum_pieces], early)
+    values, low = extend([*values, *low], [token_pieces, sum_pieces], steps[-1])
     carried = []
     for num, parts in enumerate(last):
         starts = [start for start, _ in parts]
         done = finish(
             values,
-            states,
+            [low],
             half_count,
             list(zip(starts, on_chip(*(part for _, part in parts)))),
             token_pieces,
-            sum_pieces,
+            [sum_pieces],
             queries,
             level_weight,
             near,

time: 78.8 us -> 74 us (0.939)
  starting transfers between devices: 38.9 us -> 28 us
  waiting for transfers between devices: 24.9 us -> 32 us
    ppermute x16, starting transfers between devices: 27.1 us -> 16.6 us  [move(): return lax.ppermute(part, 'ctx', route)]
    ppermute x16, waiting for transfers between devices: 20.5 us -> 24.7 us  [move(): return lax.ppermute(part, 'ctx', route)]
    ppermute x11 -> x9, waiting for transfers between devices: 4.4 us -> 7.34 us  [from_partner(): return lax.ppermute(block, axis, route)]
    ppermute x2 -> x0, starting transfers between devices: 1.33 us -> none  [body(): sent = lax.ppermute(sent, 'ctx', route)]
    ppermute x11 -> x9, starting transfers between devices: 10.5 us -> 11.4 us  [from_partner(): return lax.ppermute(block, axis, route)]
    pallas_call x5 -> x4, Pallas kernels: 5.7 us -> 5.26 us  [extend(): pl.pallas_call(functools.partial(extend_kernel, [len(pieces) for pieces i...]
  transfers between devices with their start and end apart: 29 -> 25, of which waited for: 10 -> 12; matrix products, arithmetic and copies ran while one was open for 0% -> 0% of each run, Pallas kernels for 13% -> 13%
where the time goes in v1:
time: 74 us; the launch traced here: 73.9 us
  waiting for transfers between devices  32 us (43%)
  starting transfers between devices  28 us (38%)
  Pallas kernels  13.6 us (18%)
    ppermute x16, waiting for transfers between devices, move(): return lax.ppermute(part, 'ctx', route)  24.7 us
    ppermute x16, starting transfers between devices, move(): return lax.ppermute(part, 'ctx', route)  16.6 us
    ppermute x9, starting transfers between devices, from_partner(): return lax.ppermute(block, axis, route)  11.4 us
    ppermute x9, waiting for transfers between devices, from_partner(): return lax.ppermute(block, axis, route)  7.34 us
    pallas_call x4, Pallas kernels, extend(): pl.pallas_call(functools.partial(extend_kernel, [len(pieces) for pieces i...  5.26 us
    pallas_call x2, Pallas kernels, finish(): pl.pallas_call(functools.partial(finish_kernel, len(token_pieces), len(st...  3.88 us
    pallas_call x1, Pallas kernels, prepare(): pl.pallas_call(prepare_kernel, in_specs=[pl.BlockSpec(memory_space=pltpu....  2.79 us
    pallas_call x1, Pallas kernels, begin(): pl.pallas_call(begin_kernel, in_specs=[pl.BlockSpec(memory_space=pltpu.HB...  1.59 us
  transfers between devices with their start and end apart: 25, of which 12 were waited for; matrix products, arithmetic and copies ran while one was open for 0% of the time, Pallas kernels for 13%

profile of v1, /device:TPU:0, one launch (start us, length us, event | category | flops | bytes accessed | tf_op | source)
XLA Modules:
  0.0 73.9 jit_solution(10329868925841133892)
XLA Ops:
  0.0 1.6 %begin.1 = (f32[128,512]{1,0:T(8,128)S(1)}, bf16[128,512]{1,0:T(8,128)(2,1)S(1)}, bf16[512,512]{1,0:T(8,128)(2,1)S(1)}, bf16[512,256]{1,0:T(8,128)(2,1)S(1)}, bf16[512,256]{1,0:T(8,128)(2,1)S(1)}) custom-call(bf16[512,128]{1,0:T(8,128)(2,1)} %k_hbm.3, bf16[512,512]{1,0:T(8,128)(2,1)} %token_hbm.1, bf16[256,1024]{1,0:T(8,128)(2,1)} %weight_hbm.1), custom_call_target="tpu_custom_call" | custom-call | tf_op jit(solution)/shard_map/begin/pallas_call | solution.py:177
  1.6 3.1 %collective-permute-start.3 = (bf16[128,512]{1,0:T(8,128)(2,1)S(1)}, bf16[128,512]{1,0:T(8,128)(2,1)S(1)}, u32[]{:S(2)}, u32[]{:S(2)}) collective-permute-start(bf16[128,512]{1,0:T(8,128)(2,1)S(1)} %get-tuple-element.21), channel_id=1, source_target_pairs={{0,4},{4,0},{8,12},{12,8},{16,20},{20,16},{24,28},{28,24},{1,5},{5... | collective-permute-start | bytes 393224 | tf_op jit(solution)/shard_map/ppermute | solution.py:22
  4.7 3.5 %collective-permute-done.3 = bf16[128,512]{1,0:T(8,128)(2,1)S(1)} collective-permute-done((bf16[128,512]{1,0:T(8,128)(2,1)S(1)}, bf16[128,512]{1,0:T(8,128)(2,1)S(1)}, u32[]{:S(2)}, u32[]{:S(2)}) %collective-permute-start.3) | collective-permute-done | bytes 131104 | tf_op jit(solution)/shard_map/ppermute | solution.py:22
  8.2 1.9 %collective-permute-start.4 = (bf16[128,512]{1,0:T(8,128)(2,1)S(1)}, bf16[128,512]{1,0:T(8,128)(2,1)S(1)}, u32[]{:S(2)}, u32[]{:S(2)}) collective-permute-start(bf16[128,512]{1,0:T(8,128)(2,1)S(1)} %fusion), channel_id=1, source_target_pairs={{0,8},{8,0},{4,12},{12,4},{16,24},{24,16},{20,28},{28,20},{1,9},{9... | collective-permute-start | bytes 393224 | tf_op jit(solution)/shard_map/ppermute | solution.py:22
  10.0 1.5 %collective-permute-start.20 = (bf16[512,256]{1,0:T(8,128)(2,1)S(1)}, bf16[512,256]{1,0:T(8,128)(2,1)S(1)}, u32[]{:S(2)}, u32[]{:S(2)}) collective-permute-start(bf16[512,256]{1,0:T(8,128)(2,1)S(1)} %get-tuple-element.23.refs_4_), channel_id=1, source_target_pairs={{8,0},{16,8},{24,16},{28,24},{20,28},{12,20},{4,12},{0,4},{9,1},{1... | collective-permute-start | bytes 786440 | tf_op jit(solution)/shard_map/ppermute | solution.py:473
  11.6 0.5 collective-permute-start.9
  12.1 1.1 %collective-permute-start.17 = (bf16[512,256]{1,0:T(8,128)(2,1)S(1)}, bf16[512,256]{1,0:T(8,128)(2,1)S(1)}, u32[]{:S(2)}, u32[]{:S(2)}) collective-permute-start(bf16[512,256]{1,0:T(8,128)(2,1)S(1)} %get-tuple-element.25.refs_5_), channel_id=1, source_target_pairs={{0,8},{8,16},{16,24},{24,28},{28,20},{20,12},{12,4},{4,0},{1,9},{9... | collective-permute-start | bytes 786440 | tf_op jit(solution)/shard_map/ppermute | solution.py:473
  13.2 0.9 %collective-permute-start.13 = (bf16[512,256]{1,0:T(8,128)(2,1)S(1)}, bf16[512,256]{1,0:T(8,128)(2,1)S(1)}, u32[]{:S(2)}, u32[]{:S(2)}) collective-permute-start(bf16[512,256]{1,0:T(8,128)(2,1)S(1)} %get-tuple-element.25.refs_5_), channel_id=1, source_target_pairs={{8,0},{16,8},{24,16},{28,24},{20,28},{12,20},{4,12},{0,4},{9,1},{1... | collective-permute-start | bytes 786440 | tf_op jit(solution)/shard_map/ppermute | solution.py:473
  14.1 0.5 collective-permute-done.4
  14.6 1.7 %collective-permute-start.1 = (bf16[512,512]{1,0:T(8,128)(2,1)S(1)}, bf16[512,512]{1,0:T(8,128)(2,1)S(1)}, u32[]{:S(2)}, u32[]{:S(2)}) collective-permute-start(bf16[512,512]{1,0:T(8,128)(2,1)S(1)} %get-tuple-element.20.refs_0_), channel_id=1, source_target_pairs={{0,2},{2,0},{1,3},{3,1},{4,6},{6,4},{5,7},{7,5},{8,10},{10,8},{9,1... | collective-permute-start | bytes 1572872 | tf_op jit(solution)/shard_map/ppermute | solution.py:22
  16.4 3.9 %collective-permute-done.20.refs_8_ = bf16[512,256]{1,0:T(8,128)(2,1)S(1)} collective-permute-done((bf16[512,256]{1,0:T(8,128)(2,1)S(1)}, bf16[512,256]{1,0:T(8,128)(2,1)S(1)}, u32[]{:S(2)}, u32[]{:S(2)}) %collective-permute-start.20) | collective-permute-done | bytes 262176 | tf_op jit(solution)/shard_map/ppermute | solution.py:473
  20.2 2.8 %collective-permute-start.5 = (bf16[128,512]{1,0:T(8,128)(2,1)S(1)}, bf16[128,512]{1,0:T(8,128)(2,1)S(1)}, u32[]{:S(2)}, u32[]{:S(2)}) collective-permute-start(bf16[128,512]{1,0:T(8,128)(2,1)S(1)} %add_convert_fusion), channel_id=1, source_target_pairs={{0,16},{16,0},{4,20},{20,4},{8,24},{24,8},{12,28},{28,12},{1,17},{... | collective-permute-start | bytes 393224 | tf_op jit(solution)/shard_map/ppermute | solution.py:22
  23.0 0.0 collective-permute-done.9.refs_6_
  23.0 0.6 collective-permute-start.21
  23.6 1.0 %collective-permute-done.17.refs_7_ = bf16[512,256]{1,0:T(8,128)(2,1)S(1)} collective-permute-done((bf16[512,256]{1,0:T(8,128)(2,1)S(1)}, bf16[512,256]{1,0:T(8,128)(2,1)S(1)}, u32[]{:S(2)}, u32[]{:S(2)}) %collective-permute-start.17) | collective-permute-done | bytes 262176 | tf_op jit(solution)/shard_map/ppermute | solution.py:473
  24.6 0.0 collective-permute-start
  24.7 3.0 %collective-permute-done.13.refs_9_ = bf16[512,256]{1,0:T(8,128)(2,1)S(1)} collective-permute-done((bf16[512,256]{1,0:T(8,128)(2,1)S(1)}, bf16[512,256]{1,0:T(8,128)(2,1)S(1)}, u32[]{:S(2)}, u32[]{:S(2)}) %collective-permute-start.13) | collective-permute-done | bytes 262176 | tf_op jit(solution)/shard_map/ppermute | solution.py:473
  27.7 0.0 collective-permute-start.10
  27.7 3.3 %collective-permute-done.5 = bf16[128,512]{1,0:T(8,128)(2,1)S(1)} collective-permute-done((bf16[128,512]{1,0:T(8,128)(2,1)S(1)}, bf16[128,512]{1,0:T(8,128)(2,1)S(1)}, u32[]{:S(2)}, u32[]{:S(2)}) %collective-permute-start.5) | collective-permute-done | bytes 131104 | tf_op jit(solution)/shard_map/ppermute | solution.py:22
  31.0 0.4 collective-permute-start.18
  31.5 1.1 %collective-permute-done.21.refs_6_.refs_12_ = bf16[512,256]{1,0:T(8,128)(2,1)S(1)} collective-permute-done((bf16[512,256]{1,0:T(8,128)(2,1)S(1)}, bf16[512,256]{1,0:T(8,128)(2,1)S(1)}, u32[]{:S(2)}, u32[]{:S(2)}) %collective-permute-start.21) | collective-permute-done | bytes 262176 | tf_op jit(solution)/shard_map/ppermute | solution.py:473
  32.6 1.4 %collective-permute-start.7 = (bf16[384,512]{1,0:T(8,128)(2,1)S(1)}, bf16[384,512]{1,0:T(8,128)(2,1)S(1)}, u32[]{:S(2)}, u32[]{:S(2)}) collective-permute-start(bf16[384,512]{1,0:T(8,128)(2,1)S(1)} %constant_dynamic-update-slice_fusion.refs_0_.refs_4_), channel_id=1, source_target_pairs={{0,2},{2,0},{1,3},{3,1},{4,6},{6,4},{5,7},{7,5},{8,10},{10,8},{9,1... | collective-permute-start | bytes 1179656 | tf_op jit(solution)/shard_map/ppermute | solution.py:22
  34.0 2.9 %collective-permute-done.10.refs_4_.refs_10_ = bf16[512,256]{1,0:T(8,128)(2,1)S(1)} collective-permute-done((bf16[512,256]{1,0:T(8,128)(2,1)S(1)}, bf16[512,256]{1,0:T(8,128)(2,1)S(1)}, u32[]{:S(2)}, u32[]{:S(2)}) %collective-permute-start.10) | collective-permute-done | bytes 262176 | tf_op jit(solution)/shard_map/ppermute | solution.py:473
  36.9 1.5 %collective-permute-start.14 = (bf16[512,256]{1,0:T(8,128)(2,1)S(1)}, bf16[512,256]{1,0:T(8,128)(2,1)S(1)}, u32[]{:S(2)}, u32[]{:S(2)}) collective-permute-start(bf16[512,256]{1,0:T(8,128)(2,1)S(1)} %collective-permute-done.13.refs_9_), channel_id=1, source_target_pairs={{8,0},{16,8},{24,16},{28,24},{20,28},{12,20},{4,12},{0,4},{9,1},{1... | collective-permute-start | bytes 786440 | tf_op jit(solution)/shard_map/ppermute | solution.py:473
  38.3 1.9 %collective-permute-done.18.refs_5_.refs_11_ = bf16[512,256]{1,0:T(8,128)(2,1)S(1)} collective-permute-done((bf16[512,256]{1,0:T(8,128)(2,1)S(1)}, bf16[512,256]{1,0:T(8,128)(2,1)S(1)}, u32[]{:S(2)}, u32[]{:S(2)}) %collective-permute-start.18) | collective-permute-done | bytes 262176 | tf_op jit(solution)/shard_map/ppermute | solution.py:473
  40.2 1.3 %collective-permute-start.11 = (bf16[512,256]{1,0:T(8,128)(2,1)S(1)}, bf16[512,256]{1,0:T(8,128)(2,1)S(1)}, u32[]{:S(2)}, u32[]{:S(2)}) collective-permute-start(bf16[512,256]{1,0:T(8,128)(2,1)S(1)} %collective-permute-done.10.refs_4_.refs_10_), channel_id=1, source_target_pairs={{0,8},{8,16},{16,24},{24,28},{28,20},{20,12},{12,4},{4,0},{1,9},{9... | collective-permute-start | bytes 786440 | tf_op jit(solution)/shard_map/ppermute | solution.py:473
  41.5 0.0 collective-permute-done.1.refs_2_
  41.5 0.0 collective-permute-start.2
  41.5 2.3 %collective-permute-done.14.refs_7_.refs_13_ = bf16[512,256]{1,0:T(8,128)(2,1)S(1)} collective-permute-done((bf16[512,256]{1,0:T(8,128)(2,1)S(1)}, bf16[512,256]{1,0:T(8,128)(2,1)S(1)}, u32[]{:S(2)}, u32[]{:S(2)}) %collective-permute-start.14) | collective-permute-done | bytes 262176 | tf_op jit(solution)/shard_map/ppermute | solution.py:473
  43.8 2.5 %collective-permute-start.15 = (bf16[512,256]{1,0:T(8,128)(2,1)S(1)}, bf16[512,256]{1,0:T(8,128)(2,1)S(1)}, u32[]{:S(2)}, u32[]{:S(2)}) collective-permute-start(bf16[512,256]{1,0:T(8,128)(2,1)S(1)} %collective-permute-done.14.refs_7_.refs_13_), channel_id=1, source_target_pairs={{8,0},{16,8},{24,16},{28,24},{20,28},{12,20},{4,12},{0,4},{9,1},{1... | collective-permute-start | bytes 786440 | tf_op jit(solution)/shard_map/ppermute | solution.py:473
  46.3 0.5 collective-permute-start.8
  46.8 3.4 %collective-permute-done.11.refs_0_.refs_8_ = bf16[512,256]{1,0:T(8,128)(2,1)S(1)} collective-permute-done((bf16[512,256]{1,0:T(8,128)(2,1)S(1)}, bf16[512,256]{1,0:T(8,128)(2,1)S(1)}, u32[]{:S(2)}, u32[]{:S(2)}) %collective-permute-start.11) | collective-permute-done | bytes 262176 | tf_op jit(solution)/shard_map/ppermute | solution.py:473
  50.2 1.7 %collective-permute-start.22 = (bf16[512,256]{1,0:T(8,128)(2,1)S(1)}, bf16[512,256]{1,0:T(8,128)(2,1)S(1)}, u32[]{:S(2)}, u32[]{:S(2)}) collective-permute-start(bf16[512,256]{1,0:T(8,128)(2,1)S(1)} %collective-permute-done.21.refs_6_.refs_12_), channel_id=1, source_target_pairs={{8,0},{16,8},{24,16},{28,24},{20,28},{12,20},{4,12},{0,4},{9,1},{1... | collective-permute-start | bytes 786440 | tf_op jit(solution)/shard_map/ppermute | solution.py:473
  51.9 0.0 collective-permute-done.15.refs_0_.refs_11_
  51.9 0.5 collective-permute-start.19
  52.5 5.3 %collective-permute-done.22.refs_10_ = bf16[512,256]{1,0:T(8,128)(2,1)S(1)} collective-permute-done((bf16[512,256]{1,0:T(8,128)(2,1)S(1)}, bf16[512,256]{1,0:T(8,128)(2,1)S(1)}, u32[]{:S(2)}, u32[]{:S(2)}) %collective-permute-start.22) | collective-permute-done | bytes 262176 | tf_op jit(solution)/shard_map/ppermute | solution.py:473
  57.7 2.0 %collective-permute-start.24 = (bf16[256,256]{1,0:T(8,128)(2,1)S(1)}, bf16[256,256]{1,0:T(8,128)(2,1)S(1)}, u32[]{:S(2)}, u32[]{:S(2)}) collective-permute-start(bf16[256,256]{1,0:T(8,128)(2,1)S(1)} %get-tuple-element.32), channel_id=1, source_target_pairs={{8,0},{16,8},{24,16},{28,24},{20,28},{12,20},{4,12},{0,4},{9,1},{1... | collective-permute-start | bytes 393224 | tf_op jit(solution)/shard_map/ppermute | solution.py:473
  59.8 0.0 collective-permute-start.12
  59.8 2.0 %collective-permute-start.16 = (bf16[256,256]{1,0:T(8,128)(2,1)S(1)}, bf16[256,256]{1,0:T(8,128)(2,1)S(1)}, u32[]{:S(2)}, u32[]{:S(2)}) collective-permute-start(bf16[256,256]{1,0:T(8,128)(2,1)S(1)} %get-tuple-element.26), channel_id=1, source_target_pairs={{8,0},{16,8},{24,16},{28,24},{20,28},{12,20},{4,12},{0,4},{9,1},{1... | collective-permute-start | bytes 393224 | tf_op jit(solution)/shard_map/ppermute | solution.py:473
  61.8 2.8 %prepare.1 = (bf16[16,512,256]{2,1,0:T(8,128)(2,1)S(1)}, bf16[512,512]{1,0:T(8,128)(2,1)S(1)}) custom-call(bf16[512,128]{1,0:T(8,128)(2,1)} %refs_12_.3, bf16[512,128]{1,0:T(8,128)(2,1)} %k_hbm.3, f32[13,16,512]{2,1,0:T(8,128)} %refs_13_.3), custom_call_target="tpu_custom_call" | custom-call | tf_op jit(solution)/shard_map/prepare/pallas_call | solution.py:132
  64.6 1.2 %shard_map.57.refs_8_ = f32[1024,512]{1,0:T(8,128)S(1)} custom-call(bf16[512,512]{1,0:T(8,128)(2,1)S(1)} %get-tuple-element.20.refs_0_, bf16[512,512]{1,0:T(8,128)(2,1)S(1)} %collective-permute-done.refs_1_, bf16[512,512]{1,0:T(8,128)(2,1)S(1)} %collective-permute-done.1.refs_2_, bf16[512,512]{1,0:T(8,128)(2,1)S(1)} %collective-permute-done.2.refs_3_, ...), custom_call_target="tpu_custom_call" | custom-call | tf_op jit(solution)/shard_map/pallas_call | solution.py:272
  65.8 0.9 %shard_map.58.refs_12_ = f32[1024,512]{1,0:T(8,128)S(1)} custom-call(bf16[512,512]{1,0:T(8,128)(2,1)S(1)} %get-tuple-element.20.refs_0_, bf16[512,512]{1,0:T(8,128)(2,1)S(1)} %collective-permute-done.refs_1_, bf16[512,512]{1,0:T(8,128)(2,1)S(1)} %collective-permute-done.1.refs_2_, bf16[512,512]{1,0:T(8,128)(2,1)S(1)} %collective-permute-done.2.refs_3_, ...), custom_call_target="tpu_custom_call" | custom-call | tf_op jit(solution)/shard_map/pallas_call | solution.py:272
  66.7 1.8 %shard_map.59.refs_13_ = f32[1024,384]{1,0:T(8,128)S(1)} custom-call(bf16[384,512]{1,0:T(8,128)(2,1)S(1)} %constant_dynamic-update-slice_fusion.refs_0_.refs_4_, bf16[384,512]{1,0:T(8,128)(2,1)S(1)} %collective-permute-done.6.refs_1_.refs_5_, bf16[384,512]{1,0:T(8,128)(2,1)S(1)} %collective-permute-done.7.refs_2_.refs_6_, ...), custom_call_target="tpu_custom_call" | custom-call | tf_op jit(solution)/shard_map/pallas_call | solution.py:272
  68.4 0.0 copy-start
  68.4 0.0 copy-start.1
  68.5 1.5 %shard_map.60 = (f32[1024,512]{1,0:T(8,128)S(1)}, f32[1024,384]{1,0:T(8,128)S(1)}) custom-call(bf16[512,512]{1,0:T(8,128)(2,1)S(1)} %get-tuple-element.20.refs_0_, bf16[512,512]{1,0:T(8,128)(2,1)S(1)} %collective-permute-done.refs_1_, bf16[512,512]{1,0:T(8,128)(2,1)S(1)} %collective-permute-done.1.refs_2_, ...), custom_call_target="tpu_custom_call" | custom-call | tf_op jit(solution)/shard_map/pallas_call | solution.py:272
  70.0 1.6 %finish.2 = (bf16[512,256]{1,0:T(8,128)(2,1)S(1)}, bf16[512,256]{1,0:T(8,128)(2,1)S(1)}) custom-call(bf16[512,512]{1,0:T(8,128)(2,1)S(1)} %get-tuple-element.20.refs_0_, bf16[512,512]{1,0:T(8,128)(2,1)S(1)} %collective-permute-done.refs_1_, bf16[512,512]{1,0:T(8,128)(2,1)S(1)} %collective-permute-done.1.refs_2_, ...), custom_call_target="tpu_custom_call" | custom-call | tf_op jit(solution)/shard_map/finish/pallas_call | solution.py:414
  71.6 2.3 %finish.3 = bf16[512,1024]{1,0:T(8,128)(2,1)} custom-call(bf16[512,512]{1,0:T(8,128)(2,1)S(1)} %get-tuple-element.20.refs_0_, bf16[512,512]{1,0:T(8,128)(2,1)S(1)} %collective-permute-done.refs_1_, bf16[512,512]{1,0:T(8,128)(2,1)S(1)} %collective-permute-done.1.refs_2_, bf16[512,512]{1,0:T(8,128)(2,1)S(1)} %collective-permute-done.2.refs_3_, ...), custom_call_target="tpu_custom_call" | custom-call | tf_op jit(solution)/shard_map/finish/pallas_call | solution.py:414
  (21 shorter events, 0.2 us)
Async XLA Ops:
  1.6 6.6 %collective-permute-start.3 = (bf16[128,512]{1,0:T(8,128)(2,1)S(1)}, bf16[128,512]{1,0:T(8,128)(2,1)S(1)}, u32[]{:S(2)}, u32[]{:S(2)}) collective-permute-start(bf16[128,512]{1,0:T(8,128)(2,1)S(1)} %get-tuple-element.21), channel_id=1, source_target_pairs={{0,4},{4,0},{8,12},{12,8},{16,20},{20,16},{24,28},{28,24},{1,5},{5... | collective-permute-start | bytes 393224 | tf_op jit(solution)/shard_map/ppermute | solution.py:22
  8.2 6.4 %collective-permute-start.4 = (bf16[128,512]{1,0:T(8,128)(2,1)S(1)}, bf16[128,512]{1,0:T(8,128)(2,1)S(1)}, u32[]{:S(2)}, u32[]{:S(2)}) collective-permute-start(bf16[128,512]{1,0:T(8,128)(2,1)S(1)} %fusion), channel_id=1, source_target_pairs={{0,8},{8,0},{4,12},{12,4},{16,24},{24,16},{20,28},{28,20},{1,9},{9... | collective-permute-start | bytes 393224 | tf_op jit(solution)/shard_map/ppermute | solution.py:22
  10.0 10.2 %collective-permute-start.20 = (bf16[512,256]{1,0:T(8,128)(2,1)S(1)}, bf16[512,256]{1,0:T(8,128)(2,1)S(1)}, u32[]{:S(2)}, u32[]{:S(2)}) collective-permute-start(bf16[512,256]{1,0:T(8,128)(2,1)S(1)} %get-tuple-element.23.refs_4_), channel_id=1, source_target_pairs={{8,0},{16,8},{24,16},{28,24},{20,28},{12,20},{4,12},{0,4},{9,1},{1... | collective-permute-start | bytes 786440 | tf_op jit(solution)/shard_map/ppermute | solution.py:473
  11.6 11.5 %collective-permute-start.9 = (bf16[512,256]{1,0:T(8,128)(2,1)S(1)}, bf16[512,256]{1,0:T(8,128)(2,1)S(1)}, u32[]{:S(2)}, u32[]{:S(2)}) collective-permute-start(bf16[512,256]{1,0:T(8,128)(2,1)S(1)} %get-tuple-element.23.refs_4_), channel_id=1, source_target_pairs={{0,8},{8,16},{16,24},{24,28},{28,20},{20,12},{12,4},{4,0},{1,9},{9... | collective-permute-start | bytes 786440 | tf_op jit(solution)/shard_map/ppermute | solution.py:473
  12.1 12.6 %collective-permute-start.17 = (bf16[512,256]{1,0:T(8,128)(2,1)S(1)}, bf16[512,256]{1,0:T(8,128)(2,1)S(1)}, u32[]{:S(2)}, u32[]{:S(2)}) collective-permute-start(bf16[512,256]{1,0:T(8,128)(2,1)S(1)} %get-tuple-element.25.refs_5_), channel_id=1, source_target_pairs={{0,8},{8,16},{16,24},{24,28},{28,20},{20,12},{12,4},{4,0},{1,9},{9... | collective-permute-start | bytes 786440 | tf_op jit(solution)/shard_map/ppermute | solution.py:473
  13.2 14.5 %collective-permute-start.13 = (bf16[512,256]{1,0:T(8,128)(2,1)S(1)}, bf16[512,256]{1,0:T(8,128)(2,1)S(1)}, u32[]{:S(2)}, u32[]{:S(2)}) collective-permute-start(bf16[512,256]{1,0:T(8,128)(2,1)S(1)} %get-tuple-element.25.refs_5_), channel_id=1, source_target_pairs={{8,0},{16,8},{24,16},{28,24},{20,28},{12,20},{4,12},{0,4},{9,1},{1... | collective-permute-start | bytes 786440 | tf_op jit(solution)/shard_map/ppermute | solution.py:473
  14.6 26.9 %collective-permute-start.1 = (bf16[512,512]{1,0:T(8,128)(2,1)S(1)}, bf16[512,512]{1,0:T(8,128)(2,1)S(1)}, u32[]{:S(2)}, u32[]{:S(2)}) collective-permute-start(bf16[512,512]{1,0:T(8,128)(2,1)S(1)} %get-tuple-element.20.refs_0_), channel_id=1, source_target_pairs={{0,2},{2,0},{1,3},{3,1},{4,6},{6,4},{5,7},{7,5},{8,10},{10,8},{9,1... | collective-permute-start | bytes 1572872 | tf_op jit(solution)/shard_map/ppermute | solution.py:22
  20.2 10.8 %collective-permute-start.5 = (bf16[128,512]{1,0:T(8,128)(2,1)S(1)}, bf16[128,512]{1,0:T(8,128)(2,1)S(1)}, u32[]{:S(2)}, u32[]{:S(2)}) collective-permute-start(bf16[128,512]{1,0:T(8,128)(2,1)S(1)} %add_convert_fusion), channel_id=1, source_target_pairs={{0,16},{16,0},{4,20},{20,4},{8,24},{24,8},{12,28},{28,12},{1,17},{... | collective-permute-start | bytes 393224 | tf_op jit(solution)/shard_map/ppermute | solution.py:22
  23.0 9.5 %collective-permute-start.21 = (bf16[512,256]{1,0:T(8,128)(2,1)S(1)}, bf16[512,256]{1,0:T(8,128)(2,1)S(1)}, u32[]{:S(2)}, u32[]{:S(2)}) collective-permute-start(bf16[512,256]{1,0:T(8,128)(2,1)S(1)} %collective-permute-done.20.refs_8_), channel_id=1, source_target_pairs={{8,0},{16,8},{24,16},{28,24},{20,28},{12,20},{4,12},{0,4},{9,1},{1... | collective-permute-start | bytes 786440 | tf_op jit(solution)/shard_map/ppermute | solution.py:473
  24.6 21.7 %collective-permute-start = (bf16[512,512]{1,0:T(8,128)(2,1)S(1)}, bf16[512,512]{1,0:T(8,128)(2,1)S(1)}, u32[]{:S(2)}, u32[]{:S(2)}) collective-permute-start(bf16[512,512]{1,0:T(8,128)(2,1)S(1)} %get-tuple-element.20.refs_0_), channel_id=1, source_target_pairs={{0,1},{1,0},{2,3},{3,2},{4,5},{5,4},{6,7},{7,6},{8,9},{9,8},{10,11... | collective-permute-start | bytes 1572872 | tf_op jit(solution)/shard_map/ppermute | solution.py:22
  27.7 9.2 %collective-permute-start.10 = (bf16[512,256]{1,0:T(8,128)(2,1)S(1)}, bf16[512,256]{1,0:T(8,128)(2,1)S(1)}, u32[]{:S(2)}, u32[]{:S(2)}) collective-permute-start(bf16[512,256]{1,0:T(8,128)(2,1)S(1)} %collective-permute-done.9.refs_6_), channel_id=1, source_target_pairs={{0,8},{8,16},{16,24},{24,28},{28,20},{20,12},{12,4},{4,0},{1,9},{9... | collective-permute-start | bytes 786440 | tf_op jit(solution)/shard_map/ppermute | solution.py:473
  31.0 9.2 %collective-permute-start.18 = (bf16[512,256]{1,0:T(8,128)(2,1)S(1)}, bf16[512,256]{1,0:T(8,128)(2,1)S(1)}, u32[]{:S(2)}, u32[]{:S(2)}) collective-permute-start(bf16[512,256]{1,0:T(8,128)(2,1)S(1)} %collective-permute-done.17.refs_7_), channel_id=1, source_target_pairs={{0,8},{8,16},{16,24},{24,28},{28,20},{20,12},{12,4},{4,0},{1,9},{9... | collective-permute-start | bytes 786440 | tf_op jit(solution)/shard_map/ppermute | solution.py:473
  32.6 13.7 %collective-permute-start.7 = (bf16[384,512]{1,0:T(8,128)(2,1)S(1)}, bf16[384,512]{1,0:T(8,128)(2,1)S(1)}, u32[]{:S(2)}, u32[]{:S(2)}) collective-permute-start(bf16[384,512]{1,0:T(8,128)(2,1)S(1)} %constant_dynamic-update-slice_fusion.refs_0_.refs_4_), channel_id=1, source_target_pairs={{0,2},{2,0},{1,3},{3,1},{4,6},{6,4},{5,7},{7,5},{8,10},{10,8},{9,1... | collective-permute-start | bytes 1179656 | tf_op jit(solution)/shard_map/ppermute | solution.py:22
  36.9 6.9 %collective-permute-start.14 = (bf16[512,256]{1,0:T(8,128)(2,1)S(1)}, bf16[512,256]{1,0:T(8,128)(2,1)S(1)}, u32[]{:S(2)}, u32[]{:S(2)}) collective-permute-start(bf16[512,256]{1,0:T(8,128)(2,1)S(1)} %collective-permute-done.13.refs_9_), channel_id=1, source_target_pairs={{8,0},{16,8},{24,16},{28,24},{20,28},{12,20},{4,12},{0,4},{9,1},{1... | collective-permute-start | bytes 786440 | tf_op jit(solution)/shard_map/ppermute | solution.py:473
  40.2 10.0 %collective-permute-start.11 = (bf16[512,256]{1,0:T(8,128)(2,1)S(1)}, bf16[512,256]{1,0:T(8,128)(2,1)S(1)}, u32[]{:S(2)}, u32[]{:S(2)}) collective-permute-start(bf16[512,256]{1,0:T(8,128)(2,1)S(1)} %collective-permute-done.10.refs_4_.refs_10_), channel_id=1, source_target_pairs={{0,8},{8,16},{16,24},{24,28},{28,20},{20,12},{12,4},{4,0},{1,9},{9... | collective-permute-start | bytes 786440 | tf_op jit(solution)/shard_map/ppermute | solution.py:473
  41.5 18.3 %collective-permute-start.2 = (bf16[512,512]{1,0:T(8,128)(2,1)S(1)}, bf16[512,512]{1,0:T(8,128)(2,1)S(1)}, u32[]{:S(2)}, u32[]{:S(2)}) collective-permute-start(bf16[512,512]{1,0:T(8,128)(2,1)S(1)} %collective-permute-done.1.refs_2_), channel_id=1, source_target_pairs={{0,1},{1,0},{2,3},{3,2},{4,5},{5,4},{6,7},{7,6},{8,9},{9,8},{10,11... | collective-permute-start | bytes 1572872 | tf_op jit(solution)/shard_map/ppermute | solution.py:22
  43.8 8.1 %collective-permute-start.15 = (bf16[512,256]{1,0:T(8,128)(2,1)S(1)}, bf16[512,256]{1,0:T(8,128)(2,1)S(1)}, u32[]{:S(2)}, u32[]{:S(2)}) collective-permute-start(bf16[512,256]{1,0:T(8,128)(2,1)S(1)} %collective-permute-done.14.refs_7_.refs_13_), channel_id=1, source_target_pairs={{8,0},{16,8},{24,16},{28,24},{20,28},{12,20},{4,12},{0,4},{9,1},{1... | collective-permute-start | bytes 786440 | tf_op jit(solution)/shard_map/ppermute | solution.py:473
  46.3 11.4 %collective-permute-start.6 = (bf16[384,512]{1,0:T(8,128)(2,1)S(1)}, bf16[384,512]{1,0:T(8,128)(2,1)S(1)}, u32[]{:S(2)}, u32[]{:S(2)}) collective-permute-start(bf16[384,512]{1,0:T(8,128)(2,1)S(1)} %constant_dynamic-update-slice_fusion.refs_0_.refs_4_), channel_id=1, source_target_pairs={{0,1},{1,0},{2,3},{3,2},{4,5},{5,4},{6,7},{7,6},{8,9},{9,8},{10,11... | collective-permute-start | bytes 1179656 | tf_op jit(solution)/shard_map/ppermute | solution.py:22
  46.3 13.5 %collective-permute-start.8 = (bf16[384,512]{1,0:T(8,128)(2,1)S(1)}, bf16[384,512]{1,0:T(8,128)(2,1)S(1)}, u32[]{:S(2)}, u32[]{:S(2)}) collective-permute-start(bf16[384,512]{1,0:T(8,128)(2,1)S(1)} %collective-permute-done.7.refs_2_.refs_6_), channel_id=1, source_target_pairs={{0,1},{1,0},{2,3},{3,2},{4,5},{5,4},{6,7},{7,6},{8,9},{9,8},{10,11... | collective-permute-start | bytes 1179656 | tf_op jit(solution)/shard_map/ppermute | solution.py:22
  50.2 7.6 %collective-permute-start.22 = (bf16[512,256]{1,0:T(8,128)(2,1)S(1)}, bf16[512,256]{1,0:T(8,128)(2,1)S(1)}, u32[]{:S(2)}, u32[]{:S(2)}) collective-permute-start(bf16[512,256]{1,0:T(8,128)(2,1)S(1)} %collective-permute-done.21.refs_6_.refs_12_), channel_id=1, source_target_pairs={{8,0},{16,8},{24,16},{28,24},{20,28},{12,20},{4,12},{0,4},{9,1},{1... | collective-permute-start | bytes 786440 | tf_op jit(solution)/shard_map/ppermute | solution.py:473
  51.9 16.5 %collective-permute-start.19 = (bf16[512,256]{1,0:T(8,128)(2,1)S(1)}, bf16[512,256]{1,0:T(8,128)(2,1)S(1)}, u32[]{:S(2)}, u32[]{:S(2)}) collective-permute-start(bf16[512,256]{1,0:T(8,128)(2,1)S(1)} %collective-permute-done.18.refs_5_.refs_11_), channel_id=1, source_target_pairs={{0,8},{8,16},{16,24},{24,28},{28,20},{20,12},{12,4},{4,0},{1,9},{9... | collective-permute-start | bytes 786440 | tf_op jit(solution)/shard_map/ppermute | solution.py:473
  57.7 12.2 %collective-permute-start.23 = (bf16[256,256]{1,0:T(8,128)(2,1)S(1)}, bf16[256,256]{1,0:T(8,128)(2,1)S(1)}, u32[]{:S(2)}, u32[]{:S(2)}) collective-permute-start(bf16[256,256]{1,0:T(8,128)(2,1)S(1)} %get-tuple-element.31), channel_id=1, source_target_pairs={{0,8},{8,16},{16,24},{24,28},{28,20},{20,12},{12,4},{4,0},{1,9},{9... | collective-permute-start | bytes 393224 | tf_op jit(solution)/shard_map/ppermute | solution.py:473
  57.7 12.2 %collective-permute-start.24 = (bf16[256,256]{1,0:T(8,128)(2,1)S(1)}, bf16[256,256]{1,0:T(8,128)(2,1)S(1)}, u32[]{:S(2)}, u32[]{:S(2)}) collective-permute-start(bf16[256,256]{1,0:T(8,128)(2,1)S(1)} %get-tuple-element.32), channel_id=1, source_target_pairs={{8,0},{16,8},{24,16},{28,24},{20,28},{12,20},{4,12},{0,4},{9,1},{1... | collective-permute-start | bytes 393224 | tf_op jit(solution)/shard_map/ppermute | solution.py:473
  59.8 11.8 %collective-permute-start.12 = (bf16[256,256]{1,0:T(8,128)(2,1)S(1)}, bf16[256,256]{1,0:T(8,128)(2,1)S(1)}, u32[]{:S(2)}, u32[]{:S(2)}) collective-permute-start(bf16[256,256]{1,0:T(8,128)(2,1)S(1)} %get-tuple-element.24), channel_id=1, source_target_pairs={{0,8},{8,16},{16,24},{24,28},{28,20},{20,12},{12,4},{4,0},{1,9},{9... | collective-permute-start | bytes 393224 | tf_op jit(solution)/shard_map/ppermute | solution.py:473
  59.8 11.8 %collective-permute-start.16 = (bf16[256,256]{1,0:T(8,128)(2,1)S(1)}, bf16[256,256]{1,0:T(8,128)(2,1)S(1)}, u32[]{:S(2)}, u32[]{:S(2)}) collective-permute-start(bf16[256,256]{1,0:T(8,128)(2,1)S(1)} %get-tuple-element.26), channel_id=1, source_target_pairs={{8,0},{16,8},{24,16},{28,24},{20,28},{12,20},{4,12},{0,4},{9,1},{1... | collective-permute-start | bytes 393224 | tf_op jit(solution)/shard_map/ppermute | solution.py:473
  68.4 1.5 %copy-start = (f32[13,16,512]{2,1,0:T(8,128)S(1)}, f32[13,16,512]{2,1,0:T(8,128)}, u32[]{:S(2)}) copy-start(f32[13,16,512]{2,1,0:T(8,128)} %refs_13_.3) | copy-start | bytes 1277956
  68.4 1.5 %copy-start.1 = (bf16[512,128]{1,0:T(8,128)(2,1)S(1)}, bf16[512,128]{1,0:T(8,128)(2,1)}, u32[]{:S(2)}) copy-start(bf16[512,128]{1,0:T(8,128)(2,1)} %refs_12_.3) | copy-start | bytes 393220

commit v2 on v0

--- a/solution.py
+++ b/solution.py
@@ -12,13 +12,13 @@
 BF16 = jnp.bfloat16
 
 
-def from_partner(block, axis, distance, both=True):
+def from_partner(block, axis, distance):
     count = lax.axis_size(axis)
     route = []
     for low in range(count):
         high = low | 1 << distance
         if high != low and high < count:
-            route += [(low, high), (high, low)] if both else [(low, high)]
+            route += [(low, high), (high, low)]
     return lax.ppermute(block, axis, route)
 
 
@@ -303,18 +303,16 @@
     if final:
         held_ref, sems = refs.pop(), refs.pop()
 
-        def store(source, start, low):
+        def store(source, start):
             stores.append(
                 pltpu.make_async_copy(
-                    source,
-                    out_refs[0].at[low : low + source.shape[0], start : start + step],
-                    sems.at[len(stores)],
+                    source, out_refs[0].at[:, start : start + step], sems.at[len(stores)]
                 )
             )
             stores[-1].start()
 
         for start, ref in zip(carried_at, carried_refs):
-            store(ref, start, 0)
+            store(ref, start)
     length, state_rows = q_ref.shape
     near_levels = length.bit_length()
     far_levels = w_ref.shape[0] - near_levels
@@ -385,8 +383,8 @@
                     )
                     total = total + weight(level, t0, t0 + rows) * mixed
             out_ref[t0 : t0 + rows, :] = total.astype(BF16).T
-            if final:
-                store(out_ref.at[t0 : t0 + rows, :], c0, t0)
+        if final:
+            store(out_ref, c0)
     for started in stores:
         started.wait()
 
@@ -406,7 +404,7 @@
         scratch = [pltpu.VMEM((rows, depth), BF16) for rows in [length, *(s.shape[1] for s in states)]]
     starts = [start + c0 for start, part in last for c0 in range(0, part.shape[0], step)]
     if final:
-        scratch += [pltpu.SemaphoreType.DMA((width // step * (length // near[0].shape[2]),)), pltpu.VMEM((length, width), BF16)]
+        scratch += [pltpu.SemaphoreType.DMA((max(1, width // step),)), pltpu.VMEM((length, width), BF16)]
         outs = dict(
             out_shape=jax.ShapeDtypeStruct((length, width), BF16),
             out_specs=pl.BlockSpec(memory_space=pltpu.HBM),
@@ -449,7 +447,7 @@
             sent = running.astype(BF16)
         if section_bit == dev_bits - 1 and dev_bits > 1:
             break
-        partner = from_partner(sent, "ctx", section_bit, section_bit < dev_bits - 2)
+        partner = from_partner(sent, "ctx", section_bit)
         level_sums.append(partner)
         running = running + partner.astype(F32)
     if dev_bits > 1:

time: 78.8 us -> 76.8 us (0.975)
  starting transfers between devices: 38.9 us -> 36.4 us
    ppermute x16, starting transfers between devices: 27.1 us -> 24.4 us  [move(): return lax.ppermute(part, 'ctx', route)]
    ppermute x11, waiting for transfers between devices: 4.4 us -> 5.28 us  [from_partner(): return lax.ppermute(block, axis, route)]
  transfers between devices with their start and end apart: 29 -> 29, of which waited for: 10 -> 11; matrix products, arithmetic and copies ran while one was open for 0% -> 0% of each run, Pallas kernels for 13% -> 13%
where the time goes in v2:
time: 76.8 us; the launch traced here: 76.3 us
  starting transfers between devices  36.4 us (47%)
  waiting for transfers between devices  25.5 us (33%)
  Pallas kernels  14 us (18%)
    ppermute x16, starting transfers between devices, move(): return lax.ppermute(part, 'ctx', route)  24.4 us
    ppermute x16, waiting for transfers between devices, move(): return lax.ppermute(part, 'ctx', route)  20.3 us
    ppermute x11, starting transfers between devices, from_partner(): return lax.ppermute(block, axis, route)  10.7 us
    pallas_call x5, Pallas kernels, extend(): pl.pallas_call(functools.partial(extend_kernel, [len(pieces) for pieces i...  5.7 us
    ppermute x11, waiting for transfers between devices, from_partner(): return lax.ppermute(block, axis, route)  5.28 us
    pallas_call x2, Pallas kernels, finish(): pl.pallas_call(functools.partial(finish_kernel, len(token_pieces), len(st...  3.91 us
    pallas_call x1, Pallas kernels, prepare(): pl.pallas_call(prepare_kernel, in_specs=[pl.BlockSpec(memory_space=pltpu....  2.79 us
    pallas_call x1, Pallas kernels, begin(): pl.pallas_call(begin_kernel, in_specs=[pl.BlockSpec(memory_space=pltpu.HB...  1.59 us
  transfers between devices with their start and end apart: 29, of which 11 were waited for; matrix products, arithmetic and copies ran while one was open for 0% of the time, Pallas kernels for 13%

profile of v2, /device:TPU:0, one launch (start us, length us, event | category | flops | bytes accessed | tf_op | source)
XLA Modules:
  0.0 76.3 jit_solution(11465584810780085273)
XLA Ops:
  0.0 1.6 %begin.1 = (f32[128,512]{1,0:T(8,128)S(1)}, bf16[128,512]{1,0:T(8,128)(2,1)S(1)}, bf16[512,512]{1,0:T(8,128)(2,1)S(1)}, bf16[512,256]{1,0:T(8,128)(2,1)S(1)}, bf16[512,256]{1,0:T(8,128)(2,1)S(1)}) custom-call(bf16[512,128]{1,0:T(8,128)(2,1)} %k_hbm.3, bf16[512,512]{1,0:T(8,128)(2,1)} %token_hbm.1, bf16[256,1024]{1,0:T(8,128)(2,1)} %weight_hbm.1), custom_call_target="tpu_custom_call" | custom-call | tf_op jit(solution)/shard_map/begin/pallas_call | solution.py:177
  1.6 3.1 %collective-permute-start.3 = (bf16[128,512]{1,0:T(8,128)(2,1)S(1)}, bf16[128,512]{1,0:T(8,128)(2,1)S(1)}, u32[]{:S(2)}, u32[]{:S(2)}) collective-permute-start(bf16[128,512]{1,0:T(8,128)(2,1)S(1)} %get-tuple-element.21), channel_id=1, source_target_pairs={{0,4},{4,0},{8,12},{12,8},{16,20},{20,16},{24,28},{28,24},{1,5},{5... | collective-permute-start | bytes 393224 | tf_op jit(solution)/shard_map/ppermute | solution.py:22
  4.7 3.5 %collective-permute-done.3 = bf16[128,512]{1,0:T(8,128)(2,1)S(1)} collective-permute-done((bf16[128,512]{1,0:T(8,128)(2,1)S(1)}, bf16[128,512]{1,0:T(8,128)(2,1)S(1)}, u32[]{:S(2)}, u32[]{:S(2)}) %collective-permute-start.3) | collective-permute-done | bytes 131104 | tf_op jit(solution)/shard_map/ppermute | solution.py:22
  8.2 1.9 %collective-permute-start.4 = (bf16[128,512]{1,0:T(8,128)(2,1)S(1)}, bf16[128,512]{1,0:T(8,128)(2,1)S(1)}, u32[]{:S(2)}, u32[]{:S(2)}) collective-permute-start(bf16[128,512]{1,0:T(8,128)(2,1)S(1)} %fusion), channel_id=1, source_target_pairs={{0,8},{8,0},{4,12},{12,4},{16,24},{24,16},{20,28},{28,20},{1,9},{9... | collective-permute-start | bytes 393224 | tf_op jit(solution)/shard_map/ppermute | solution.py:22
  10.0 1.5 %collective-permute-start.24 = (bf16[512,256]{1,0:T(8,128)(2,1)S(1)}, bf16[512,256]{1,0:T(8,128)(2,1)S(1)}, u32[]{:S(2)}, u32[]{:S(2)}) collective-permute-start(bf16[512,256]{1,0:T(8,128)(2,1)S(1)} %get-tuple-element.23.refs_4_), channel_id=1, source_target_pairs={{8,0},{16,8},{24,16},{28,24},{20,28},{12,20},{4,12},{0,4},{9,1},{1... | collective-permute-start | bytes 786440 | tf_op jit(solution)/shard_map/ppermute | solution.py:485
  11.6 0.5 collective-permute-start.13
  12.1 1.1 %collective-permute-start.21 = (bf16[512,256]{1,0:T(8,128)(2,1)S(1)}, bf16[512,256]{1,0:T(8,128)(2,1)S(1)}, u32[]{:S(2)}, u32[]{:S(2)}) collective-permute-start(bf16[512,256]{1,0:T(8,128)(2,1)S(1)} %get-tuple-element.25.refs_5_), channel_id=1, source_target_pairs={{0,8},{8,16},{16,24},{24,28},{28,20},{20,12},{12,4},{4,0},{1,9},{9... | collective-permute-start | bytes 786440 | tf_op jit(solution)/shard_map/ppermute | solution.py:485
  13.2 0.9 %collective-permute-start.17 = (bf16[512,256]{1,0:T(8,128)(2,1)S(1)}, bf16[512,256]{1,0:T(8,128)(2,1)S(1)}, u32[]{:S(2)}, u32[]{:S(2)}) collective-permute-start(bf16[512,256]{1,0:T(8,128)(2,1)S(1)} %get-tuple-element.25.refs_5_), channel_id=1, source_target_pairs={{8,0},{16,8},{24,16},{28,24},{20,28},{12,20},{4,12},{0,4},{9,1},{1... | collective-permute-start | bytes 786440 | tf_op jit(solution)/shard_map/ppermute | solution.py:485
  14.1 0.5 collective-permute-done.4
  14.7 0.7 collective-permute-start.8
  15.4 4.9 %collective-permute-done.24.refs_8_ = bf16[512,256]{1,0:T(8,128)(2,1)S(1)} collective-permute-done((bf16[512,256]{1,0:T(8,128)(2,1)S(1)}, bf16[512,256]{1,0:T(8,128)(2,1)S(1)}, u32[]{:S(2)}, u32[]{:S(2)}) %collective-permute-start.24) | collective-permute-done | bytes 262176 | tf_op jit(solution)/shard_map/ppermute | solution.py:485
  20.2 1.7 %collective-permute-start.6 = (bf16[256,512]{1,0:T(8,128)(2,1)S(1)}, bf16[256,512]{1,0:T(8,128)(2,1)S(1)}, u32[]{:S(2)}, u32[]{:S(2)}) collective-permute-start(bf16[256,512]{1,0:T(8,128)(2,1)S(1)} %constant_dynamic-update-slice_fusion.refs_0_.refs_4_), channel_id=1, source_target_pairs={{0,2},{2,0},{1,3},{3,1},{4,6},{6,4},{5,7},{7,5},{8,10},{10,8},{9,1... | collective-permute-start | bytes 786440 | tf_op jit(solution)/shard_map/ppermute | solution.py:22
  22.0 0.7 collective-permute-start.9
  22.6 0.0 collective-permute-done.13.refs_6_
  22.6 0.1 collective-permute-start.5
  22.7 1.1 %collective-permute-done.21.refs_7_ = bf16[512,256]{1,0:T(8,128)(2,1)S(1)} collective-permute-done((bf16[512,256]{1,0:T(8,128)(2,1)S(1)}, bf16[512,256]{1,0:T(8,128)(2,1)S(1)}, u32[]{:S(2)}, u32[]{:S(2)}) %collective-permute-start.21) | collective-permute-done | bytes 262176 | tf_op jit(solution)/shard_map/ppermute | solution.py:485
  23.8 1.5 %collective-permute-start.1 = (bf16[512,512]{1,0:T(8,128)(2,1)S(1)}, bf16[512,512]{1,0:T(8,128)(2,1)S(1)}, u32[]{:S(2)}, u32[]{:S(2)}) collective-permute-start(bf16[512,512]{1,0:T(8,128)(2,1)S(1)} %get-tuple-element.20.refs_0_), channel_id=1, source_target_pairs={{0,2},{2,0},{1,3},{3,1},{4,6},{6,4},{5,7},{7,5},{8,10},{10,8},{9,1... | collective-permute-start | bytes 1572872 | tf_op jit(solution)/shard_map/ppermute | solution.py:22
  25.3 2.4 %collective-permute-start.25 = (bf16[512,256]{1,0:T(8,128)(2,1)S(1)}, bf16[512,256]{1,0:T(8,128)(2,1)S(1)}, u32[]{:S(2)}, u32[]{:S(2)}) collective-permute-start(bf16[512,256]{1,0:T(8,128)(2,1)S(1)} %collective-permute-done.24.refs_8_), channel_id=1, source_target_pairs={{8,0},{16,8},{24,16},{28,24},{20,28},{12,20},{4,12},{0,4},{9,1},{1... | collective-permute-start | bytes 786440 | tf_op jit(solution)/shard_map/ppermute | solution.py:485
  27.7 0.3 collective-permute-done.6.refs_2_.refs_6_
  28.0 0.6 collective-permute-start.14
  28.6 3.7 %collective-permute-start.22 = (bf16[512,256]{1,0:T(8,128)(2,1)S(1)}, bf16[512,256]{1,0:T(8,128)(2,1)S(1)}, u32[]{:S(2)}, u32[]{:S(2)}) collective-permute-start(bf16[512,256]{1,0:T(8,128)(2,1)S(1)} %collective-permute-done.21.refs_7_), channel_id=1, source_target_pairs={{0,8},{8,16},{16,24},{24,28},{28,20},{20,12},{12,4},{4,0},{1,9},{9... | collective-permute-start | bytes 786440 | tf_op jit(solution)/shard_map/ppermute | solution.py:485
  32.3 2.7 %collective-permute-done.25.refs_6_.refs_12_ = bf16[512,256]{1,0:T(8,128)(2,1)S(1)} collective-permute-done((bf16[512,256]{1,0:T(8,128)(2,1)S(1)}, bf16[512,256]{1,0:T(8,128)(2,1)S(1)}, u32[]{:S(2)}, u32[]{:S(2)}) %collective-permute-start.25) | collective-permute-done | bytes 262176 | tf_op jit(solution)/shard_map/ppermute | solution.py:485
  35.0 0.8 %collective-permute-start.18 = (bf16[512,256]{1,0:T(8,128)(2,1)S(1)}, bf16[512,256]{1,0:T(8,128)(2,1)S(1)}, u32[]{:S(2)}, u32[]{:S(2)}) collective-permute-start(bf16[512,256]{1,0:T(8,128)(2,1)S(1)} %collective-permute-done.17.refs_9_), channel_id=1, source_target_pairs={{8,0},{16,8},{24,16},{28,24},{20,28},{12,20},{4,12},{0,4},{9,1},{1... | collective-permute-start | bytes 786440 | tf_op jit(solution)/shard_map/ppermute | solution.py:485
  35.8 1.4 %collective-permute-done.14.refs_4_.refs_10_ = bf16[512,256]{1,0:T(8,128)(2,1)S(1)} collective-permute-done((bf16[512,256]{1,0:T(8,128)(2,1)S(1)}, bf16[512,256]{1,0:T(8,128)(2,1)S(1)}, u32[]{:S(2)}, u32[]{:S(2)}) %collective-permute-start.14) | collective-permute-done | bytes 262176 | tf_op jit(solution)/shard_map/ppermute | solution.py:485
  37.2 1.8 %collective-permute-start.15 = (bf16[512,256]{1,0:T(8,128)(2,1)S(1)}, bf16[512,256]{1,0:T(8,128)(2,1)S(1)}, u32[]{:S(2)}, u32[]{:S(2)}) collective-permute-start(bf16[512,256]{1,0:T(8,128)(2,1)S(1)} %collective-permute-done.14.refs_4_.refs_10_), channel_id=1, source_target_pairs={{0,8},{8,16},{16,24},{24,28},{28,20},{20,12},{12,4},{4,0},{1,9},{9... | collective-permute-start | bytes 786440 | tf_op jit(solution)/shard_map/ppermute | solution.py:485
  39.1 3.8 %collective-permute-done.22.refs_5_.refs_11_ = bf16[512,256]{1,0:T(8,128)(2,1)S(1)} collective-permute-done((bf16[512,256]{1,0:T(8,128)(2,1)S(1)}, bf16[512,256]{1,0:T(8,128)(2,1)S(1)}, u32[]{:S(2)}, u32[]{:S(2)}) %collective-permute-start.22) | collective-permute-done | bytes 262176 | tf_op jit(solution)/shard_map/ppermute | solution.py:485
  42.8 2.0 %collective-permute-start.11 = (bf16[128,512]{1,0:T(8,128)(2,1)S(1)}, bf16[128,512]{1,0:T(8,128)(2,1)S(1)}, u32[]{:S(2)}, u32[]{:S(2)}) collective-permute-start(bf16[128,512]{1,0:T(8,128)(2,1)S(1)} %add.11.refs_0_.refs_8_), channel_id=1, source_target_pairs={{0,2},{2,0},{1,3},{3,1},{4,6},{6,4},{5,7},{7,5},{8,10},{10,8},{9,1... | collective-permute-start | bytes 393224 | tf_op jit(solution)/shard_map/ppermute | solution.py:22
  44.8 0.5 collective-permute-start.10
  45.3 1.6 %collective-permute-start.19 = (bf16[512,256]{1,0:T(8,128)(2,1)S(1)}, bf16[512,256]{1,0:T(8,128)(2,1)S(1)}, u32[]{:S(2)}, u32[]{:S(2)}) collective-permute-start(bf16[512,256]{1,0:T(8,128)(2,1)S(1)} %collective-permute-done.18.refs_7_.refs_13_), channel_id=1, source_target_pairs={{8,0},{16,8},{24,16},{28,24},{20,28},{12,20},{4,12},{0,4},{9,1},{1... | collective-permute-start | bytes 786440 | tf_op jit(solution)/shard_map/ppermute | solution.py:485
  46.9 0.9 %collective-permute-done.11.refs_2_.refs_10_ = bf16[128,512]{1,0:T(8,128)(2,1)S(1)} collective-permute-done((bf16[128,512]{1,0:T(8,128)(2,1)S(1)}, bf16[128,512]{1,0:T(8,128)(2,1)S(1)}, u32[]{:S(2)}, u32[]{:S(2)}) %collective-permute-start.11) | collective-permute-done | bytes 131104 | tf_op jit(solution)/shard_map/ppermute | solution.py:22
  47.8 3.1 %collective-permute-start.26 = (bf16[512,256]{1,0:T(8,128)(2,1)S(1)}, bf16[512,256]{1,0:T(8,128)(2,1)S(1)}, u32[]{:S(2)}, u32[]{:S(2)}) collective-permute-start(bf16[512,256]{1,0:T(8,128)(2,1)S(1)} %collective-permute-done.25.refs_6_.refs_12_), channel_id=1, source_target_pairs={{8,0},{16,8},{24,16},{28,24},{20,28},{12,20},{4,12},{0,4},{9,1},{1... | collective-permute-start | bytes 786440 | tf_op jit(solution)/shard_map/ppermute | solution.py:485
  50.9 0.0 collective-permute-done.15.refs_0_.refs_8_.refs_14_
  50.9 3.6 %collective-permute-done.19.refs_0_.refs_11_.refs_17_ = bf16[512,256]{1,0:T(8,128)(2,1)S(1)} collective-permute-done((bf16[512,256]{1,0:T(8,128)(2,1)S(1)}, bf16[512,256]{1,0:T(8,128)(2,1)S(1)}, u32[]{:S(2)}, u32[]{:S(2)}) %collective-permute-start.19) | collective-permute-done | bytes 262176 | tf_op jit(solution)/shard_map/ppermute | solution.py:485
  54.6 1.8 %collective-permute-start.27 = (bf16[256,256]{1,0:T(8,128)(2,1)S(1)}, bf16[256,256]{1,0:T(8,128)(2,1)S(1)}, u32[]{:S(2)}, u32[]{:S(2)}) collective-permute-start(bf16[256,256]{1,0:T(8,128)(2,1)S(1)} %get-tuple-element.31), channel_id=1, source_target_pairs={{0,8},{8,16},{16,24},{24,28},{28,20},{20,12},{12,4},{4,0},{1,9},{9... | collective-permute-start | bytes 393224 | tf_op jit(solution)/shard_map/ppermute | solution.py:485
  56.4 2.8 %collective-permute-done.26.refs_10_.refs_16_ = bf16[512,256]{1,0:T(8,128)(2,1)S(1)} collective-permute-done((bf16[512,256]{1,0:T(8,128)(2,1)S(1)}, bf16[512,256]{1,0:T(8,128)(2,1)S(1)}, u32[]{:S(2)}, u32[]{:S(2)}) %collective-permute-start.26) | collective-permute-done | bytes 262176 | tf_op jit(solution)/shard_map/ppermute | solution.py:485
  59.2 2.0 %collective-permute-start.28 = (bf16[256,256]{1,0:T(8,128)(2,1)S(1)}, bf16[256,256]{1,0:T(8,128)(2,1)S(1)}, u32[]{:S(2)}, u32[]{:S(2)}) collective-permute-start(bf16[256,256]{1,0:T(8,128)(2,1)S(1)} %get-tuple-element.32), channel_id=1, source_target_pairs={{8,0},{16,8},{24,16},{28,24},{20,28},{12,20},{4,12},{0,4},{9,1},{1... | collective-permute-start | bytes 393224 | tf_op jit(solution)/shard_map/ppermute | solution.py:485
  61.2 0.1 collective-permute-start.16
  61.3 2.5 %collective-permute-start.20 = (bf16[256,256]{1,0:T(8,128)(2,1)S(1)}, bf16[256,256]{1,0:T(8,128)(2,1)S(1)}, u32[]{:S(2)}, u32[]{:S(2)}) collective-permute-start(bf16[256,256]{1,0:T(8,128)(2,1)S(1)} %get-tuple-element.26), channel_id=1, source_target_pairs={{8,0},{16,8},{24,16},{28,24},{20,28},{12,20},{4,12},{0,4},{9,1},{1... | collective-permute-start | bytes 393224 | tf_op jit(solution)/shard_map/ppermute | solution.py:485
  63.8 2.8 %prepare.1 = (bf16[16,512,256]{2,1,0:T(8,128)(2,1)S(1)}, bf16[512,512]{1,0:T(8,128)(2,1)S(1)}) custom-call(bf16[512,128]{1,0:T(8,128)(2,1)} %refs_17_.3, bf16[512,128]{1,0:T(8,128)(2,1)} %k_hbm.3, f32[13,16,512]{2,1,0:T(8,128)} %refs_18_.3), custom_call_target="tpu_custom_call" | custom-call | tf_op jit(solution)/shard_map/prepare/pallas_call | solution.py:132
  66.6 1.1 %shard_map.59.refs_13_ = f32[1024,256]{1,0:T(8,128)S(1)} custom-call(bf16[256,512]{1,0:T(8,128)(2,1)S(1)} %constant_dynamic-update-slice_fusion.refs_0_.refs_4_, bf16[256,512]{1,0:T(8,128)(2,1)S(1)} %collective-permute-done.5.refs_1_.refs_5_, bf16[256,512]{1,0:T(8,128)(2,1)S(1)} %collective-permute-done.6.refs_2_.refs_6_, ...), custom_call_target="tpu_custom_call" | custom-call | tf_op jit(solution)/shard_map/pallas_call | solution.py:272
  67.7 1.4 %shard_map.61.refs_16_ = f32[1024,128]{1,0:T(8,128)S(1)} custom-call(bf16[128,512]{1,0:T(8,128)(2,1)S(1)} %add.11.refs_0_.refs_8_, bf16[128,512]{1,0:T(8,128)(2,1)S(1)} %collective-permute-done.10.refs_1_.refs_9_, bf16[128,512]{1,0:T(8,128)(2,1)S(1)} %collective-permute-done.11.refs_2_.refs_10_, ...), custom_call_target="tpu_custom_call" | custom-call | tf_op jit(solution)/shard_map/pallas_call | solution.py:272
  69.1 1.2 %shard_map.57.refs_8_ = f32[1024,512]{1,0:T(8,128)S(1)} custom-call(bf16[512,512]{1,0:T(8,128)(2,1)S(1)} %get-tuple-element.20.refs_0_, bf16[512,512]{1,0:T(8,128)(2,1)S(1)} %collective-permute-done.refs_1_, bf16[512,512]{1,0:T(8,128)(2,1)S(1)} %collective-permute-done.1.refs_2_, bf16[512,512]{1,0:T(8,128)(2,1)S(1)} %collective-permute-done.2.refs_3_, ...), custom_call_target="tpu_custom_call" | custom-call | tf_op jit(solution)/shard_map/pallas_call | solution.py:272
  70.3 0.9 %shard_map.58.refs_12_ = f32[1024,512]{1,0:T(8,128)S(1)} custom-call(bf16[512,512]{1,0:T(8,128)(2,1)S(1)} %get-tuple-element.20.refs_0_, bf16[512,512]{1,0:T(8,128)(2,1)S(1)} %collective-permute-done.refs_1_, bf16[512,512]{1,0:T(8,128)(2,1)S(1)} %collective-permute-done.1.refs_2_, bf16[512,512]{1,0:T(8,128)(2,1)S(1)} %collective-permute-done.2.refs_3_, ...), custom_call_target="tpu_custom_call" | custom-call | tf_op jit(solution)/shard_map/pallas_call | solution.py:272
  71.2 0.0 copy-start
  71.2 0.0 copy-start.1
  71.2 1.2 %shard_map.60 = (f32[1024,512]{1,0:T(8,128)S(1)}, f32[1024,256]{1,0:T(8,128)S(1)}) custom-call(bf16[512,512]{1,0:T(8,128)(2,1)S(1)} %get-tuple-element.20.refs_0_, bf16[512,512]{1,0:T(8,128)(2,1)S(1)} %collective-permute-done.refs_1_, bf16[512,512]{1,0:T(8,128)(2,1)S(1)} %collective-permute-done.1.refs_2_, ...), custom_call_target="tpu_custom_call" | custom-call | tf_op jit(solution)/shard_map/pallas_call | solution.py:272
  72.4 1.6 %finish.2 = (bf16[512,256]{1,0:T(8,128)(2,1)S(1)}, bf16[512,256]{1,0:T(8,128)(2,1)S(1)}) custom-call(bf16[512,512]{1,0:T(8,128)(2,1)S(1)} %get-tuple-element.20.refs_0_, bf16[512,512]{1,0:T(8,128)(2,1)S(1)} %collective-permute-done.refs_1_, bf16[512,512]{1,0:T(8,128)(2,1)S(1)} %collective-permute-done.1.refs_2_, ...), custom_call_target="tpu_custom_call" | custom-call | tf_op jit(solution)/shard_map/finish/pallas_call | solution.py:414
  74.0 2.3 %finish.3 = bf16[512,1024]{1,0:T(8,128)(2,1)} custom-call(bf16[512,512]{1,0:T(8,128)(2,1)S(1)} %get-tuple-element.20.refs_0_, bf16[512,512]{1,0:T(8,128)(2,1)S(1)} %collective-permute-done.refs_1_, bf16[512,512]{1,0:T(8,128)(2,1)S(1)} %collective-permute-done.1.refs_2_, bf16[512,512]{1,0:T(8,128)(2,1)S(1)} %collective-permute-done.2.refs_3_, ...), custom_call_target="tpu_custom_call" | custom-call | tf_op jit(solution)/shard_map/finish/pallas_call | solution.py:414
  (30 shorter events, 0.2 us)
Async XLA Ops:
  1.6 6.6 %collective-permute-start.3 = (bf16[128,512]{1,0:T(8,128)(2,1)S(1)}, bf16[128,512]{1,0:T(8,128)(2,1)S(1)}, u32[]{:S(2)}, u32[]{:S(2)}) collective-permute-start(bf16[128,512]{1,0:T(8,128)(2,1)S(1)} %get-tuple-element.21), channel_id=1, source_target_pairs={{0,4},{4,0},{8,12},{12,8},{16,20},{20,16},{24,28},{28,24},{1,5},{5... | collective-permute-start | bytes 393224 | tf_op jit(solution)/shard_map/ppermute | solution.py:22
  8.2 6.4 %collective-permute-start.4 = (bf16[128,512]{1,0:T(8,128)(2,1)S(1)}, bf16[128,512]{1,0:T(8,128)(2,1)S(1)}, u32[]{:S(2)}, u32[]{:S(2)}) collective-permute-start(bf16[128,512]{1,0:T(8,128)(2,1)S(1)} %fusion), channel_id=1, source_target_pairs={{0,8},{8,0},{4,12},{12,4},{16,24},{24,16},{20,28},{28,20},{1,9},{9... | collective-permute-start | bytes 393224 | tf_op jit(solution)/shard_map/ppermute | solution.py:22
  10.0 10.2 %collective-permute-start.24 = (bf16[512,256]{1,0:T(8,128)(2,1)S(1)}, bf16[512,256]{1,0:T(8,128)(2,1)S(1)}, u32[]{:S(2)}, u32[]{:S(2)}) collective-permute-start(bf16[512,256]{1,0:T(8,128)(2,1)S(1)} %get-tuple-element.23.refs_4_), channel_id=1, source_target_pairs={{8,0},{16,8},{24,16},{28,24},{20,28},{12,20},{4,12},{0,4},{9,1},{1... | collective-permute-start | bytes 786440 | tf_op jit(solution)/shard_map/ppermute | solution.py:485
  11.6 11.1 %collective-permute-start.13 = (bf16[512,256]{1,0:T(8,128)(2,1)S(1)}, bf16[512,256]{1,0:T(8,128)(2,1)S(1)}, u32[]{:S(2)}, u32[]{:S(2)}) collective-permute-start(bf16[512,256]{1,0:T(8,128)(2,1)S(1)} %get-tuple-element.23.refs_4_), channel_id=1, source_target_pairs={{0,8},{8,16},{16,24},{24,28},{28,20},{20,12},{12,4},{4,0},{1,9},{9... | collective-permute-start | bytes 786440 | tf_op jit(solution)/shard_map/ppermute | solution.py:485
  12.1 11.7 %collective-permute-start.21 = (bf16[512,256]{1,0:T(8,128)(2,1)S(1)}, bf16[512,256]{1,0:T(8,128)(2,1)S(1)}, u32[]{:S(2)}, u32[]{:S(2)}) collective-permute-start(bf16[512,256]{1,0:T(8,128)(2,1)S(1)} %get-tuple-element.25.refs_5_), channel_id=1, source_target_pairs={{0,8},{8,16},{16,24},{24,28},{28,20},{20,12},{12,4},{4,0},{1,9},{9... | collective-permute-start | bytes 786440 | tf_op jit(solution)/shard_map/ppermute | solution.py:485
  13.2 12.1 %collective-permute-start.17 = (bf16[512,256]{1,0:T(8,128)(2,1)S(1)}, bf16[512,256]{1,0:T(8,128)(2,1)S(1)}, u32[]{:S(2)}, u32[]{:S(2)}) collective-permute-start(bf16[512,256]{1,0:T(8,128)(2,1)S(1)} %get-tuple-element.25.refs_5_), channel_id=1, source_target_pairs={{8,0},{16,8},{24,16},{28,24},{20,28},{12,20},{4,12},{0,4},{9,1},{1... | collective-permute-start | bytes 786440 | tf_op jit(solution)/shard_map/ppermute | solution.py:485
  14.7 7.3 %collective-permute-start.8 = (bf16[128,512]{1,0:T(8,128)(2,1)S(1)}, bf16[128,512]{1,0:T(8,128)(2,1)S(1)}, u32[]{:S(2)}, u32[]{:S(2)}) collective-permute-start(bf16[128,512]{1,0:T(8,128)(2,1)S(1)} %add_convert_fusion), channel_id=1, source_target_pairs={{8,16},{12,20},{9,17},{13,21},{10,18},{14,22},{11,19},{15,23}} | collective-permute-start | bytes 393224 | tf_op jit(solution)/shard_map/ppermute | solution.py:457
  20.2 7.8 %collective-permute-start.6 = (bf16[256,512]{1,0:T(8,128)(2,1)S(1)}, bf16[256,512]{1,0:T(8,128)(2,1)S(1)}, u32[]{:S(2)}, u32[]{:S(2)}) collective-permute-start(bf16[256,512]{1,0:T(8,128)(2,1)S(1)} %constant_dynamic-update-slice_fusion.refs_0_.refs_4_), channel_id=1, source_target_pairs={{0,2},{2,0},{1,3},{3,1},{4,6},{6,4},{5,7},{7,5},{8,10},{10,8},{9,1... | collective-permute-start | bytes 786440 | tf_op jit(solution)/shard_map/ppermute | solution.py:22
  22.0 5.7 %collective-permute-start.9 = (bf16[128,512]{1,0:T(8,128)(2,1)S(1)}, bf16[128,512]{1,0:T(8,128)(2,1)S(1)}, u32[]{:S(2)}, u32[]{:S(2)}) collective-permute-start(bf16[128,512]{1,0:T(8,128)(2,1)S(1)} %collective-permute-done.8), channel_id=1, source_target_pairs={{16,24},{20,28},{17,25},{21,29},{18,26},{22,30},{19,27},{23,31}} | collective-permute-start | bytes 393224 | tf_op jit(solution)/shard_map/ppermute | solution.py:457
  22.6 6.0 %collective-permute-start.5 = (bf16[256,512]{1,0:T(8,128)(2,1)S(1)}, bf16[256,512]{1,0:T(8,128)(2,1)S(1)}, u32[]{:S(2)}, u32[]{:S(2)}) collective-permute-start(bf16[256,512]{1,0:T(8,128)(2,1)S(1)} %constant_dynamic-update-slice_fusion.refs_0_.refs_4_), channel_id=1, source_target_pairs={{0,1},{1,0},{2,3},{3,2},{4,5},{5,4},{6,7},{7,6},{8,9},{9,8},{10,11... | collective-permute-start | bytes 786440 | tf_op jit(solution)/shard_map/ppermute | solution.py:22
  23.8 21.0 %collective-permute-start.1 = (bf16[512,512]{1,0:T(8,128)(2,1)S(1)}, bf16[512,512]{1,0:T(8,128)(2,1)S(1)}, u32[]{:S(2)}, u32[]{:S(2)}) collective-permute-start(bf16[512,512]{1,0:T(8,128)(2,1)S(1)} %get-tuple-element.20.refs_0_), channel_id=1, source_target_pairs={{0,2},{2,0},{1,3},{3,1},{4,6},{6,4},{5,7},{7,5},{8,10},{10,8},{9,1... | collective-permute-start | bytes 1572872 | tf_op jit(solution)/shard_map/ppermute | solution.py:22
  25.3 9.7 %collective-permute-start.25 = (bf16[512,256]{1,0:T(8,128)(2,1)S(1)}, bf16[512,256]{1,0:T(8,128)(2,1)S(1)}, u32[]{:S(2)}, u32[]{:S(2)}) collective-permute-start(bf16[512,256]{1,0:T(8,128)(2,1)S(1)} %collective-permute-done.24.refs_8_), channel_id=1, source_target_pairs={{8,0},{16,8},{24,16},{28,24},{20,28},{12,20},{4,12},{0,4},{9,1},{1... | collective-permute-start | bytes 786440 | tf_op jit(solution)/shard_map/ppermute | solution.py:485
  27.7 17.6 %collective-permute-start = (bf16[512,512]{1,0:T(8,128)(2,1)S(1)}, bf16[512,512]{1,0:T(8,128)(2,1)S(1)}, u32[]{:S(2)}, u32[]{:S(2)}) collective-permute-start(bf16[512,512]{1,0:T(8,128)(2,1)S(1)} %get-tuple-element.20.refs_0_), channel_id=1, source_target_pairs={{0,1},{1,0},{2,3},{3,2},{4,5},{5,4},{6,7},{7,6},{8,9},{9,8},{10,11... | collective-permute-start | bytes 1572872 | tf_op jit(solution)/shard_map/ppermute | solution.py:22
  28.0 9.2 %collective-permute-start.14 = (bf16[512,256]{1,0:T(8,128)(2,1)S(1)}, bf16[512,256]{1,0:T(8,128)(2,1)S(1)}, u32[]{:S(2)}, u32[]{:S(2)}) collective-permute-start(bf16[512,256]{1,0:T(8,128)(2,1)S(1)} %collective-permute-done.13.refs_6_), channel_id=1, source_target_pairs={{0,8},{8,16},{16,24},{24,28},{28,20},{20,12},{12,4},{4,0},{1,9},{9... | collective-permute-start | bytes 786440 | tf_op jit(solution)/shard_map/ppermute | solution.py:485
  28.6 14.2 %collective-permute-start.22 = (bf16[512,256]{1,0:T(8,128)(2,1)S(1)}, bf16[512,256]{1,0:T(8,128)(2,1)S(1)}, u32[]{:S(2)}, u32[]{:S(2)}) collective-permute-start(bf16[512,256]{1,0:T(8,128)(2,1)S(1)} %collective-permute-done.21.refs_7_), channel_id=1, source_target_pairs={{0,8},{8,16},{16,24},{24,28},{28,20},{20,12},{12,4},{4,0},{1,9},{9... | collective-permute-start | bytes 786440 | tf_op jit(solution)/shard_map/ppermute | solution.py:485
  35.0 9.8 %collective-permute-start.18 = (bf16[512,256]{1,0:T(8,128)(2,1)S(1)}, bf16[512,256]{1,0:T(8,128)(2,1)S(1)}, u32[]{:S(2)}, u32[]{:S(2)}) collective-permute-start(bf16[512,256]{1,0:T(8,128)(2,1)S(1)} %collective-permute-done.17.refs_9_), channel_id=1, source_target_pairs={{8,0},{16,8},{24,16},{28,24},{20,28},{12,20},{4,12},{0,4},{9,1},{1... | collective-permute-start | bytes 786440 | tf_op jit(solution)/shard_map/ppermute | solution.py:485
  37.2 13.7 %collective-permute-start.15 = (bf16[512,256]{1,0:T(8,128)(2,1)S(1)}, bf16[512,256]{1,0:T(8,128)(2,1)S(1)}, u32[]{:S(2)}, u32[]{:S(2)}) collective-permute-start(bf16[512,256]{1,0:T(8,128)(2,1)S(1)} %collective-permute-done.14.refs_4_.refs_10_), channel_id=1, source_target_pairs={{0,8},{8,16},{16,24},{24,28},{28,20},{20,12},{12,4},{4,0},{1,9},{9... | collective-permute-start | bytes 786440 | tf_op jit(solution)/shard_map/ppermute | solution.py:485
  42.8 5.0 %collective-permute-start.11 = (bf16[128,512]{1,0:T(8,128)(2,1)S(1)}, bf16[128,512]{1,0:T(8,128)(2,1)S(1)}, u32[]{:S(2)}, u32[]{:S(2)}) collective-permute-start(bf16[128,512]{1,0:T(8,128)(2,1)S(1)} %add.11.refs_0_.refs_8_), channel_id=1, source_target_pairs={{0,2},{2,0},{1,3},{3,1},{4,6},{6,4},{5,7},{7,5},{8,10},{10,8},{9,1... | collective-permute-start | bytes 393224 | tf_op jit(solution)/shard_map/ppermute | solution.py:22
  44.8 24.3 %collective-permute-start.2 = (bf16[512,512]{1,0:T(8,128)(2,1)S(1)}, bf16[512,512]{1,0:T(8,128)(2,1)S(1)}, u32[]{:S(2)}, u32[]{:S(2)}) collective-permute-start(bf16[512,512]{1,0:T(8,128)(2,1)S(1)} %collective-permute-done.1.refs_2_), channel_id=1, source_target_pairs={{0,1},{1,0},{2,3},{3,2},{4,5},{5,4},{6,7},{7,6},{8,9},{9,8},{10,11... | collective-permute-start | bytes 1572872 | tf_op jit(solution)/shard_map/ppermute | solution.py:22
  44.8 3.0 %collective-permute-start.10 = (bf16[128,512]{1,0:T(8,128)(2,1)S(1)}, bf16[128,512]{1,0:T(8,128)(2,1)S(1)}, u32[]{:S(2)}, u32[]{:S(2)}) collective-permute-start(bf16[128,512]{1,0:T(8,128)(2,1)S(1)} %add.11.refs_0_.refs_8_), channel_id=1, source_target_pairs={{0,1},{1,0},{2,3},{3,2},{4,5},{5,4},{6,7},{7,6},{8,9},{9,8},{10,11... | collective-permute-start | bytes 393224 | tf_op jit(solution)/shard_map/ppermute | solution.py:22
  45.3 9.2 %collective-permute-start.19 = (bf16[512,256]{1,0:T(8,128)(2,1)S(1)}, bf16[512,256]{1,0:T(8,128)(2,1)S(1)}, u32[]{:S(2)}, u32[]{:S(2)}) collective-permute-start(bf16[512,256]{1,0:T(8,128)(2,1)S(1)} %collective-permute-done.18.refs_7_.refs_13_), channel_id=1, source_target_pairs={{8,0},{16,8},{24,16},{28,24},{20,28},{12,20},{4,12},{0,4},{9,1},{1... | collective-permute-start | bytes 786440 | tf_op jit(solution)/shard_map/ppermute | solution.py:485
  47.8 6.8 %collective-permute-start.7 = (bf16[256,512]{1,0:T(8,128)(2,1)S(1)}, bf16[256,512]{1,0:T(8,128)(2,1)S(1)}, u32[]{:S(2)}, u32[]{:S(2)}) collective-permute-start(bf16[256,512]{1,0:T(8,128)(2,1)S(1)} %collective-permute-done.6.refs_2_.refs_6_), channel_id=1, source_target_pairs={{0,1},{1,0},{2,3},{3,2},{4,5},{5,4},{6,7},{7,6},{8,9},{9,8},{10,11... | collective-permute-start | bytes 786440 | tf_op jit(solution)/shard_map/ppermute | solution.py:22
  47.8 11.4 %collective-permute-start.26 = (bf16[512,256]{1,0:T(8,128)(2,1)S(1)}, bf16[512,256]{1,0:T(8,128)(2,1)S(1)}, u32[]{:S(2)}, u32[]{:S(2)}) collective-permute-start(bf16[512,256]{1,0:T(8,128)(2,1)S(1)} %collective-permute-done.25.refs_6_.refs_12_), channel_id=1, source_target_pairs={{8,0},{16,8},{24,16},{28,24},{20,28},{12,20},{4,12},{0,4},{9,1},{1... | collective-permute-start | bytes 786440 | tf_op jit(solution)/shard_map/ppermute | solution.py:485
  50.9 10.3 %collective-permute-start.23 = (bf16[512,256]{1,0:T(8,128)(2,1)S(1)}, bf16[512,256]{1,0:T(8,128)(2,1)S(1)}, u32[]{:S(2)}, u32[]{:S(2)}) collective-permute-start(bf16[512,256]{1,0:T(8,128)(2,1)S(1)} %collective-permute-done.22.refs_5_.refs_11_), channel_id=1, source_target_pairs={{0,8},{8,16},{16,24},{24,28},{28,20},{20,12},{12,4},{4,0},{1,9},{9... | collective-permute-start | bytes 786440 | tf_op jit(solution)/shard_map/ppermute | solution.py:485
  54.5 6.8 %collective-permute-start.12 = (bf16[128,512]{1,0:T(8,128)(2,1)S(1)}, bf16[128,512]{1,0:T(8,128)(2,1)S(1)}, u32[]{:S(2)}, u32[]{:S(2)}) collective-permute-start(bf16[128,512]{1,0:T(8,128)(2,1)S(1)} %collective-permute-done.11.refs_2_.refs_10_), channel_id=1, source_target_pairs={{0,1},{1,0},{2,3},{3,2},{4,5},{5,4},{6,7},{7,6},{8,9},{9,8},{10,11... | collective-permute-start | bytes 393224 | tf_op jit(solution)/shard_map/ppermute | solution.py:22
  54.6 17.8 %collective-permute-start.27 = (bf16[256,256]{1,0:T(8,128)(2,1)S(1)}, bf16[256,256]{1,0:T(8,128)(2,1)S(1)}, u32[]{:S(2)}, u32[]{:S(2)}) collective-permute-start(bf16[256,256]{1,0:T(8,128)(2,1)S(1)} %get-tuple-element.31), channel_id=1, source_target_pairs={{0,8},{8,16},{16,24},{24,28},{28,20},{20,12},{12,4},{4,0},{1,9},{9... | collective-permute-start | bytes 393224 | tf_op jit(solution)/shard_map/ppermute | solution.py:485
  59.2 13.1 %collective-permute-start.28 = (bf16[256,256]{1,0:T(8,128)(2,1)S(1)}, bf16[256,256]{1,0:T(8,128)(2,1)S(1)}, u32[]{:S(2)}, u32[]{:S(2)}) collective-permute-start(bf16[256,256]{1,0:T(8,128)(2,1)S(1)} %get-tuple-element.32), channel_id=1, source_target_pairs={{8,0},{16,8},{24,16},{28,24},{20,28},{12,20},{4,12},{0,4},{9,1},{1... | collective-permute-start | bytes 393224 | tf_op jit(solution)/shard_map/ppermute | solution.py:485
  61.2 12.8 %collective-permute-start.16 = (bf16[256,256]{1,0:T(8,128)(2,1)S(1)}, bf16[256,256]{1,0:T(8,128)(2,1)S(1)}, u32[]{:S(2)}, u32[]{:S(2)}) collective-permute-start(bf16[256,256]{1,0:T(8,128)(2,1)S(1)} %get-tuple-element.24), channel_id=1, source_target_pairs={{0,8},{8,16},{16,24},{24,28},{28,20},{20,12},{12,4},{4,0},{1,9},{9... | collective-permute-start | bytes 393224 | tf_op jit(solution)/shard_map/ppermute | solution.py:485
  61.3 12.7 %collective-permute-start.20 = (bf16[256,256]{1,0:T(8,128)(2,1)S(1)}, bf16[256,256]{1,0:T(8,128)(2,1)S(1)}, u32[]{:S(2)}, u32[]{:S(2)}) collective-permute-start(bf16[256,256]{1,0:T(8,128)(2,1)S(1)} %get-tuple-element.26), channel_id=1, source_target_pairs={{8,0},{16,8},{24,16},{28,24},{20,28},{12,20},{4,12},{0,4},{9,1},{1... | collective-permute-start | bytes 393224 | tf_op jit(solution)/shard_map/ppermute | solution.py:485
  71.2 1.2 %copy-start = (f32[13,16,512]{2,1,0:T(8,128)S(1)}, f32[13,16,512]{2,1,0:T(8,128)}, u32[]{:S(2)}) copy-start(f32[13,16,512]{2,1,0:T(8,128)} %refs_18_.3) | copy-start | bytes 1277956
  71.2 1.2 %copy-start.1 = (bf16[512,128]{1,0:T(8,128)(2,1)S(1)}, bf16[512,128]{1,0:T(8,128)(2,1)}, u32[]{:S(2)}) copy-start(bf16[512,128]{1,0:T(8,128)(2,1)} %refs_17_.3) | copy-start | bytes 393220

commit v3 on v2

--- a/solution.py
+++ b/solution.py
@@ -499,9 +499,8 @@
         values = extend(values, [token_pieces], steps[step])
     early = [part for parts in steps[:-1] for part in parts]
     low = extend([], sum_pieces[:1], early)
-    values, low = extend([*values, *low], [token_pieces, sum_pieces[0]], steps[-1])
-    top = [extend([], [pieces], early + steps[-1])[0] for pieces in sum_pieces[1:]]
-    states = [low, *top]
+    top = [extend([], [pieces], early)[0] for pieces in sum_pieces[1:]]
+    values, *states = extend([*values, *low, *top], [token_pieces, *sum_pieces], steps[-1])
     carried = []
     for num, parts in enumerate(last):
         starts = [start for start, _ in parts]

time: 76.8 us -> 79.3 us (1.033)
  waiting for transfers between devices: 25.5 us -> 32.1 us
  starting transfers between devices: 36.4 us -> 32.7 us
    ppermute x11, waiting for transfers between devices: 5.28 us -> 13.4 us  [from_partner(): return lax.ppermute(block, axis, route)]
    ppermute x16, starting transfers between devices: 24.4 us -> 21.5 us  [move(): return lax.ppermute(part, 'ctx', route)]
    ppermute x16, waiting for transfers between devices: 20.3 us -> 18.7 us  [move(): return lax.ppermute(part, 'ctx', route)]
    ppermute x11, starting transfers between devices: 10.7 us -> 9.89 us  [from_partner(): return lax.ppermute(block, axis, route)]
  transfers between devices with their start and end apart: 29 -> 29, of which waited for: 11 -> 10; matrix products, arithmetic and copies ran while one was open for 0% -> 0% of each run, Pallas kernels for 13% -> 13%
where the time goes in v3:
time: 79.3 us; the launch traced here: 79.2 us
  starting transfers between devices  32.7 us (41%)
  waiting for transfers between devices  32.1 us (40%)
  Pallas kernels  14 us (18%)
    ppermute x16, starting transfers between devices, move(): return lax.ppermute(part, 'ctx', route)  21.5 us
    ppermute x16, waiting for transfers between devices, move(): return lax.ppermute(part, 'ctx', route)  18.7 us
    ppermute x11, waiting for transfers between devices, from_partner(): return lax.ppermute(block, axis, route)  13.4 us
    ppermute x11, starting transfers between devices, from_partner(): return lax.ppermute(block, axis, route)  9.89 us
    pallas_call x5, Pallas kernels, extend(): pl.pallas_call(functools.partial(extend_kernel, [len(pieces) for pieces i...  5.64 us
    pallas_call x2, Pallas kernels, finish(): pl.pallas_call(functools.partial(finish_kernel, len(token_pieces), len(st...  3.92 us
    pallas_call x1, Pallas kernels, prepare(): pl.pallas_call(prepare_kernel, in_specs=[pl.BlockSpec(memory_space=pltpu....  2.8 us
    pallas_call x1, Pallas kernels, begin(): pl.pallas_call(begin_kernel, in_specs=[pl.BlockSpec(memory_space=pltpu.HB...  1.59 us
  transfers between devices with their start and end apart: 29, of which 10 were waited for; matrix products, arithmetic and copies ran while one was open for 0% of the time, Pallas kernels for 13%

profile of v3, /device:TPU:0, one launch (start us, length us, event | category | flops | bytes accessed | tf_op | source)
XLA Modules:
  0.0 79.2 jit_solution(9339525256419580801)
XLA Ops:
  0.0 1.6 %begin.1 = (f32[128,512]{1,0:T(8,128)S(1)}, bf16[128,512]{1,0:T(8,128)(2,1)S(1)}, bf16[512,512]{1,0:T(8,128)(2,1)S(1)}, bf16[512,256]{1,0:T(8,128)(2,1)S(1)}, bf16[512,256]{1,0:T(8,128)(2,1)S(1)}) custom-call(bf16[512,128]{1,0:T(8,128)(2,1)} %k_hbm.3, bf16[512,512]{1,0:T(8,128)(2,1)} %token_hbm.1, bf16[256,1024]{1,0:T(8,128)(2,1)} %weight_hbm.1), custom_call_target="tpu_custom_call" | custom-call | tf_op jit(solution)/shard_map/begin/pallas_call | solution.py:177
  1.6 3.1 %collective-permute-start.3 = (bf16[128,512]{1,0:T(8,128)(2,1)S(1)}, bf16[128,512]{1,0:T(8,128)(2,1)S(1)}, u32[]{:S(2)}, u32[]{:S(2)}) collective-permute-start(bf16[128,512]{1,0:T(8,128)(2,1)S(1)} %get-tuple-element.22), channel_id=1, source_target_pairs={{0,4},{4,0},{8,12},{12,8},{16,20},{20,16},{24,28},{28,24},{1,5},{5... | collective-permute-start | bytes 393224 | tf_op jit(solution)/shard_map/ppermute | solution.py:22
  4.7 3.5 %collective-permute-done.3 = bf16[128,512]{1,0:T(8,128)(2,1)S(1)} collective-permute-done((bf16[128,512]{1,0:T(8,128)(2,1)S(1)}, bf16[128,512]{1,0:T(8,128)(2,1)S(1)}, u32[]{:S(2)}, u32[]{:S(2)}) %collective-permute-start.3) | collective-permute-done | bytes 131104 | tf_op jit(solution)/shard_map/ppermute | solution.py:22
  8.2 1.9 %collective-permute-start.4 = (bf16[128,512]{1,0:T(8,128)(2,1)S(1)}, bf16[128,512]{1,0:T(8,128)(2,1)S(1)}, u32[]{:S(2)}, u32[]{:S(2)}) collective-permute-start(bf16[128,512]{1,0:T(8,128)(2,1)S(1)} %fusion), channel_id=1, source_target_pairs={{0,8},{8,0},{4,12},{12,4},{16,24},{24,16},{20,28},{28,20},{1,9},{9... | collective-permute-start | bytes 393224 | tf_op jit(solution)/shard_map/ppermute | solution.py:22
  10.1 1.5 %collective-permute-start.24 = (bf16[512,256]{1,0:T(8,128)(2,1)S(1)}, bf16[512,256]{1,0:T(8,128)(2,1)S(1)}, u32[]{:S(2)}, u32[]{:S(2)}) collective-permute-start(bf16[512,256]{1,0:T(8,128)(2,1)S(1)} %get-tuple-element.24.refs_4_), channel_id=1, source_target_pairs={{8,0},{16,8},{24,16},{28,24},{20,28},{12,20},{4,12},{0,4},{9,1},{1... | collective-permute-start | bytes 786440 | tf_op jit(solution)/shard_map/ppermute | solution.py:485
  11.6 3.0 %collective-permute-done.4 = bf16[128,512]{1,0:T(8,128)(2,1)S(1)} collective-permute-done((bf16[128,512]{1,0:T(8,128)(2,1)S(1)}, bf16[128,512]{1,0:T(8,128)(2,1)S(1)}, u32[]{:S(2)}, u32[]{:S(2)}) %collective-permute-start.4) | collective-permute-done | bytes 131104 | tf_op jit(solution)/shard_map/ppermute | solution.py:22
  14.6 0.1 add_convert_fusion
  14.7 0.7 collective-permute-start.8
  15.4 4.7 %collective-permute-start.13 = (bf16[512,256]{1,0:T(8,128)(2,1)S(1)}, bf16[512,256]{1,0:T(8,128)(2,1)S(1)}, u32[]{:S(2)}, u32[]{:S(2)}) collective-permute-start(bf16[512,256]{1,0:T(8,128)(2,1)S(1)} %get-tuple-element.24.refs_4_), channel_id=1, source_target_pairs={{0,8},{8,16},{16,24},{24,28},{28,20},{20,12},{12,4},{4,0},{1,9},{9... | collective-permute-start | bytes 786440 | tf_op jit(solution)/shard_map/ppermute | solution.py:485
  20.0 0.1 collective-permute-start.21
  20.1 2.0 %collective-permute-start.17 = (bf16[512,256]{1,0:T(8,128)(2,1)S(1)}, bf16[512,256]{1,0:T(8,128)(2,1)S(1)}, u32[]{:S(2)}, u32[]{:S(2)}) collective-permute-start(bf16[512,256]{1,0:T(8,128)(2,1)S(1)} %get-tuple-element.26.refs_5_), channel_id=1, source_target_pairs={{8,0},{16,8},{24,16},{28,24},{20,28},{12,20},{4,12},{0,4},{9,1},{1... | collective-permute-start | bytes 786440 | tf_op jit(solution)/shard_map/ppermute | solution.py:485
  22.0 0.0 collective-permute-done.24.refs_8_
  22.1 1.5 %collective-permute-start.1 = (bf16[512,512]{1,0:T(8,128)(2,1)S(1)}, bf16[512,512]{1,0:T(8,128)(2,1)S(1)}, u32[]{:S(2)}, u32[]{:S(2)}) collective-permute-start(bf16[512,512]{1,0:T(8,128)(2,1)S(1)} %get-tuple-element.21.refs_0_), channel_id=1, source_target_pairs={{0,2},{2,0},{1,3},{3,1},{4,6},{6,4},{5,7},{7,5},{8,10},{10,8},{9,1... | collective-permute-start | bytes 1572872 | tf_op jit(solution)/shard_map/ppermute | solution.py:22
  23.5 0.7 collective-permute-start.9
  24.3 0.5 collective-permute-done.13.refs_6_
  24.7 1.5 %collective-permute-start.6 = (bf16[256,512]{1,0:T(8,128)(2,1)S(1)}, bf16[256,512]{1,0:T(8,128)(2,1)S(1)}, u32[]{:S(2)}, u32[]{:S(2)}) collective-permute-start(bf16[256,512]{1,0:T(8,128)(2,1)S(1)} %constant_dynamic-update-slice_fusion.refs_0_.refs_4_), channel_id=1, source_target_pairs={{0,2},{2,0},{1,3},{3,1},{4,6},{6,4},{5,7},{7,5},{8,10},{10,8},{9,1... | collective-permute-start | bytes 786440 | tf_op jit(solution)/shard_map/ppermute | solution.py:22
  26.2 1.3 %collective-permute-done.21.refs_7_ = bf16[512,256]{1,0:T(8,128)(2,1)S(1)} collective-permute-done((bf16[512,256]{1,0:T(8,128)(2,1)S(1)}, bf16[512,256]{1,0:T(8,128)(2,1)S(1)}, u32[]{:S(2)}, u32[]{:S(2)}) %collective-permute-start.21) | collective-permute-done | bytes 262176 | tf_op jit(solution)/shard_map/ppermute | solution.py:485
  27.5 2.3 %collective-permute-start.25 = (bf16[512,256]{1,0:T(8,128)(2,1)S(1)}, bf16[512,256]{1,0:T(8,128)(2,1)S(1)}, u32[]{:S(2)}, u32[]{:S(2)}) collective-permute-start(bf16[512,256]{1,0:T(8,128)(2,1)S(1)} %collective-permute-done.24.refs_8_), channel_id=1, source_target_pairs={{8,0},{16,8},{24,16},{28,24},{20,28},{12,20},{4,12},{0,4},{9,1},{1... | collective-permute-start | bytes 786440 | tf_op jit(solution)/shard_map/ppermute | solution.py:485
  29.8 0.2 collective-permute-start
  30.0 6.8 %collective-permute-done.6.refs_2_.refs_6_ = bf16[256,512]{1,0:T(8,128)(2,1)S(1)} collective-permute-done((bf16[256,512]{1,0:T(8,128)(2,1)S(1)}, bf16[256,512]{1,0:T(8,128)(2,1)S(1)}, u32[]{:S(2)}, u32[]{:S(2)}) %collective-permute-start.6) | collective-permute-done | bytes 262176 | tf_op jit(solution)/shard_map/ppermute | solution.py:22
  36.8 0.3 collective-permute-start.14
  37.2 2.0 %collective-permute-start.22 = (bf16[512,256]{1,0:T(8,128)(2,1)S(1)}, bf16[512,256]{1,0:T(8,128)(2,1)S(1)}, u32[]{:S(2)}, u32[]{:S(2)}) collective-permute-start(bf16[512,256]{1,0:T(8,128)(2,1)S(1)} %collective-permute-done.21.refs_7_), channel_id=1, source_target_pairs={{0,8},{8,16},{16,24},{24,28},{28,20},{20,12},{12,4},{4,0},{1,9},{9... | collective-permute-start | bytes 786440 | tf_op jit(solution)/shard_map/ppermute | solution.py:485
  39.2 0.1 collective-permute-start.2
  39.3 3.9 %collective-permute-done.14.refs_4_.refs_10_ = bf16[512,256]{1,0:T(8,128)(2,1)S(1)} collective-permute-done((bf16[512,256]{1,0:T(8,128)(2,1)S(1)}, bf16[512,256]{1,0:T(8,128)(2,1)S(1)}, u32[]{:S(2)}, u32[]{:S(2)}) %collective-permute-start.14) | collective-permute-done | bytes 262176 | tf_op jit(solution)/shard_map/ppermute | solution.py:485
  43.2 1.5 %collective-permute-start.11 = (bf16[128,512]{1,0:T(8,128)(2,1)S(1)}, bf16[128,512]{1,0:T(8,128)(2,1)S(1)}, u32[]{:S(2)}, u32[]{:S(2)}) collective-permute-start(bf16[128,512]{1,0:T(8,128)(2,1)S(1)} %add.11.refs_0_.refs_8_), channel_id=1, source_target_pairs={{0,2},{2,0},{1,3},{3,1},{4,6},{6,4},{5,7},{7,5},{8,10},{10,8},{9,1... | collective-permute-start | bytes 393224 | tf_op jit(solution)/shard_map/ppermute | solution.py:22
  44.7 3.6 %collective-permute-done.22.refs_5_.refs_11_ = bf16[512,256]{1,0:T(8,128)(2,1)S(1)} collective-permute-done((bf16[512,256]{1,0:T(8,128)(2,1)S(1)}, bf16[512,256]{1,0:T(8,128)(2,1)S(1)}, u32[]{:S(2)}, u32[]{:S(2)}) %collective-permute-start.22) | collective-permute-done | bytes 262176 | tf_op jit(solution)/shard_map/ppermute | solution.py:485
  48.3 0.4 collective-permute-start.15
  48.7 1.6 %collective-permute-start.19 = (bf16[512,256]{1,0:T(8,128)(2,1)S(1)}, bf16[512,256]{1,0:T(8,128)(2,1)S(1)}, u32[]{:S(2)}, u32[]{:S(2)}) collective-permute-start(bf16[512,256]{1,0:T(8,128)(2,1)S(1)} %collective-permute-done.18.refs_7_.refs_13_), channel_id=1, source_target_pairs={{8,0},{16,8},{24,16},{28,24},{20,28},{12,20},{4,12},{0,4},{9,1},{1... | collective-permute-start | bytes 786440 | tf_op jit(solution)/shard_map/ppermute | solution.py:485
  50.4 0.2 collective-permute-start.7
  50.5 1.1 %collective-permute-start.26 = (bf16[512,256]{1,0:T(8,128)(2,1)S(1)}, bf16[512,256]{1,0:T(8,128)(2,1)S(1)}, u32[]{:S(2)}, u32[]{:S(2)}) collective-permute-start(bf16[512,256]{1,0:T(8,128)(2,1)S(1)} %collective-permute-done.25.refs_6_.refs_12_), channel_id=1, source_target_pairs={{8,0},{16,8},{24,16},{28,24},{20,28},{12,20},{4,12},{0,4},{9,1},{1... | collective-permute-start | bytes 786440 | tf_op jit(solution)/shard_map/ppermute | solution.py:485
  51.6 3.5 %collective-permute-done.15.refs_0_.refs_12_ = bf16[512,256]{1,0:T(8,128)(2,1)S(1)} collective-permute-done((bf16[512,256]{1,0:T(8,128)(2,1)S(1)}, bf16[512,256]{1,0:T(8,128)(2,1)S(1)}, u32[]{:S(2)}, u32[]{:S(2)}) %collective-permute-start.15) | collective-permute-done | bytes 262176 | tf_op jit(solution)/shard_map/ppermute | solution.py:485
  55.1 0.5 collective-permute-start.23
  55.6 2.8 %collective-permute-done.19.refs_0_.refs_15_ = bf16[512,256]{1,0:T(8,128)(2,1)S(1)} collective-permute-done((bf16[512,256]{1,0:T(8,128)(2,1)S(1)}, bf16[512,256]{1,0:T(8,128)(2,1)S(1)}, u32[]{:S(2)}, u32[]{:S(2)}) %collective-permute-start.19) | collective-permute-done | bytes 262176 | tf_op jit(solution)/shard_map/ppermute | solution.py:485
  58.5 2.1 %collective-permute-start.27 = (bf16[256,256]{1,0:T(8,128)(2,1)S(1)}, bf16[256,256]{1,0:T(8,128)(2,1)S(1)}, u32[]{:S(2)}, u32[]{:S(2)}) collective-permute-start(bf16[256,256]{1,0:T(8,128)(2,1)S(1)} %get-tuple-element.33), channel_id=1, source_target_pairs={{0,8},{8,16},{16,24},{24,28},{28,20},{20,12},{12,4},{4,0},{1,9},{9... | collective-permute-start | bytes 393224 | tf_op jit(solution)/shard_map/ppermute | solution.py:485
  60.5 3.2 %collective-permute-done.26.refs_14_ = bf16[512,256]{1,0:T(8,128)(2,1)S(1)} collective-permute-done((bf16[512,256]{1,0:T(8,128)(2,1)S(1)}, bf16[512,256]{1,0:T(8,128)(2,1)S(1)}, u32[]{:S(2)}, u32[]{:S(2)}) %collective-permute-start.26) | collective-permute-done | bytes 262176 | tf_op jit(solution)/shard_map/ppermute | solution.py:485
  63.8 0.8 %collective-permute-start.28 = (bf16[256,256]{1,0:T(8,128)(2,1)S(1)}, bf16[256,256]{1,0:T(8,128)(2,1)S(1)}, u32[]{:S(2)}, u32[]{:S(2)}) collective-permute-start(bf16[256,256]{1,0:T(8,128)(2,1)S(1)} %get-tuple-element.34), channel_id=1, source_target_pairs={{8,0},{16,8},{24,16},{28,24},{20,28},{12,20},{4,12},{0,4},{9,1},{1... | collective-permute-start | bytes 393224 | tf_op jit(solution)/shard_map/ppermute | solution.py:485
  64.6 1.2 %collective-permute-start.16 = (bf16[256,256]{1,0:T(8,128)(2,1)S(1)}, bf16[256,256]{1,0:T(8,128)(2,1)S(1)}, u32[]{:S(2)}, u32[]{:S(2)}) collective-permute-start(bf16[256,256]{1,0:T(8,128)(2,1)S(1)} %get-tuple-element.25), channel_id=1, source_target_pairs={{0,8},{8,16},{16,24},{24,28},{28,20},{20,12},{12,4},{4,0},{1,9},{9... | collective-permute-start | bytes 393224 | tf_op jit(solution)/shard_map/ppermute | solution.py:485
  65.8 0.8 %collective-permute-start.20 = (bf16[256,256]{1,0:T(8,128)(2,1)S(1)}, bf16[256,256]{1,0:T(8,128)(2,1)S(1)}, u32[]{:S(2)}, u32[]{:S(2)}) collective-permute-start(bf16[256,256]{1,0:T(8,128)(2,1)S(1)} %get-tuple-element.27), channel_id=1, source_target_pairs={{8,0},{16,8},{24,16},{28,24},{20,28},{12,20},{4,12},{0,4},{9,1},{1... | collective-permute-start | bytes 393224 | tf_op jit(solution)/shard_map/ppermute | solution.py:485
  66.7 2.8 %prepare.1 = (bf16[16,512,256]{2,1,0:T(8,128)(2,1)S(1)}, bf16[512,512]{1,0:T(8,128)(2,1)S(1)}) custom-call(bf16[512,128]{1,0:T(8,128)(2,1)} %refs_17_.3, bf16[512,128]{1,0:T(8,128)(2,1)} %k_hbm.3, f32[13,16,512]{2,1,0:T(8,128)} %refs_18_.3), custom_call_target="tpu_custom_call" | custom-call | tf_op jit(solution)/shard_map/prepare/pallas_call | solution.py:132
  69.5 1.1 %shard_map.59.refs_17_ = f32[1024,256]{1,0:T(8,128)S(1)} custom-call(bf16[256,512]{1,0:T(8,128)(2,1)S(1)} %constant_dynamic-update-slice_fusion.refs_0_.refs_4_, bf16[256,512]{1,0:T(8,128)(2,1)S(1)} %collective-permute-done.5.refs_1_.refs_5_, bf16[256,512]{1,0:T(8,128)(2,1)S(1)} %collective-permute-done.6.refs_2_.refs_6_, ...), custom_call_target="tpu_custom_call" | custom-call | tf_op jit(solution)/shard_map/pallas_call | solution.py:272
  70.6 1.0 %shard_map.60.refs_18_ = f32[1024,128]{1,0:T(8,128)S(1)} custom-call(bf16[128,512]{1,0:T(8,128)(2,1)S(1)} %add.11.refs_0_.refs_8_, bf16[128,512]{1,0:T(8,128)(2,1)S(1)} %collective-permute-done.10.refs_1_.refs_9_, bf16[128,512]{1,0:T(8,128)(2,1)S(1)} %collective-permute-done.11.refs_2_.refs_10_, ...), custom_call_target="tpu_custom_call" | custom-call | tf_op jit(solution)/shard_map/pallas_call | solution.py:272
  71.6 1.2 %shard_map.57.refs_8_ = f32[1024,512]{1,0:T(8,128)S(1)} custom-call(bf16[512,512]{1,0:T(8,128)(2,1)S(1)} %get-tuple-element.21.refs_0_, bf16[512,512]{1,0:T(8,128)(2,1)S(1)} %collective-permute-done.refs_1_, bf16[512,512]{1,0:T(8,128)(2,1)S(1)} %collective-permute-done.1.refs_2_, bf16[512,512]{1,0:T(8,128)(2,1)S(1)} %collective-permute-done.2.refs_3_, ...), custom_call_target="tpu_custom_call" | custom-call | tf_op jit(solution)/shard_map/pallas_call | solution.py:272
  72.8 0.9 %shard_map.58.refs_16_ = f32[1024,512]{1,0:T(8,128)S(1)} custom-call(bf16[512,512]{1,0:T(8,128)(2,1)S(1)} %get-tuple-element.21.refs_0_, bf16[512,512]{1,0:T(8,128)(2,1)S(1)} %collective-permute-done.refs_1_, bf16[512,512]{1,0:T(8,128)(2,1)S(1)} %collective-permute-done.1.refs_2_, bf16[512,512]{1,0:T(8,128)(2,1)S(1)} %collective-permute-done.2.refs_3_, ...), custom_call_target="tpu_custom_call" | custom-call | tf_op jit(solution)/shard_map/pallas_call | solution.py:272
  73.7 0.0 copy-start
  73.7 0.0 copy-start.1
  73.7 1.5 %shard_map.61 = (f32[1024,512]{1,0:T(8,128)S(1)}, f32[1024,256]{1,0:T(8,128)S(1)}, f32[1024,128]{1,0:T(8,128)S(1)}) custom-call(bf16[512,512]{1,0:T(8,128)(2,1)S(1)} %get-tuple-element.21.refs_0_, bf16[512,512]{1,0:T(8,128)(2,1)S(1)} %collective-permute-done.refs_1_, bf16[512,512]{1,0:T(8,128)(2,1)S(1)} %collective-permute-done.1.refs_2_, ...), custom_call_target="tpu_custom_call" | custom-call | tf_op jit(solution)/shard_map/pallas_call | solution.py:272
  75.2 1.6 %finish.2 = (bf16[512,256]{1,0:T(8,128)(2,1)S(1)}, bf16[512,256]{1,0:T(8,128)(2,1)S(1)}) custom-call(bf16[512,512]{1,0:T(8,128)(2,1)S(1)} %get-tuple-element.21.refs_0_, bf16[512,512]{1,0:T(8,128)(2,1)S(1)} %collective-permute-done.refs_1_, bf16[512,512]{1,0:T(8,128)(2,1)S(1)} %collective-permute-done.1.refs_2_, ...), custom_call_target="tpu_custom_call" | custom-call | tf_op jit(solution)/shard_map/finish/pallas_call | solution.py:414
  76.8 2.3 %finish.3 = bf16[512,1024]{1,0:T(8,128)(2,1)} custom-call(bf16[512,512]{1,0:T(8,128)(2,1)S(1)} %get-tuple-element.21.refs_0_, bf16[512,512]{1,0:T(8,128)(2,1)S(1)} %collective-permute-done.refs_1_, bf16[512,512]{1,0:T(8,128)(2,1)S(1)} %collective-permute-done.1.refs_2_, bf16[512,512]{1,0:T(8,128)(2,1)S(1)} %collective-permute-done.2.refs_3_, ...), custom_call_target="tpu_custom_call" | custom-call | tf_op jit(solution)/shard_map/finish/pallas_call | solution.py:414
  (30 shorter events, 0.2 us)
Async XLA Ops:
  1.6 6.6 %collective-permute-start.3 = (bf16[128,512]{1,0:T(8,128)(2,1)S(1)}, bf16[128,512]{1,0:T(8,128)(2,1)S(1)}, u32[]{:S(2)}, u32[]{:S(2)}) collective-permute-start(bf16[128,512]{1,0:T(8,128)(2,1)S(1)} %get-tuple-element.22), channel_id=1, source_target_pairs={{0,4},{4,0},{8,12},{12,8},{16,20},{20,16},{24,28},{28,24},{1,5},{5... | collective-permute-start | bytes 393224 | tf_op jit(solution)/shard_map/ppermute | solution.py:22
  8.2 6.4 %collective-permute-start.4 = (bf16[128,512]{1,0:T(8,128)(2,1)S(1)}, bf16[128,512]{1,0:T(8,128)(2,1)S(1)}, u32[]{:S(2)}, u32[]{:S(2)}) collective-permute-start(bf16[128,512]{1,0:T(8,128)(2,1)S(1)} %fusion), channel_id=1, source_target_pairs={{0,8},{8,0},{4,12},{12,4},{16,24},{24,16},{20,28},{28,20},{1,9},{9... | collective-permute-start | bytes 393224 | tf_op jit(solution)/shard_map/ppermute | solution.py:22
  10.1 12.0 %collective-permute-start.24 = (bf16[512,256]{1,0:T(8,128)(2,1)S(1)}, bf16[512,256]{1,0:T(8,128)(2,1)S(1)}, u32[]{:S(2)}, u32[]{:S(2)}) collective-permute-start(bf16[512,256]{1,0:T(8,128)(2,1)S(1)} %get-tuple-element.24.refs_4_), channel_id=1, source_target_pairs={{8,0},{16,8},{24,16},{28,24},{20,28},{12,20},{4,12},{0,4},{9,1},{1... | collective-permute-start | bytes 786440 | tf_op jit(solution)/shard_map/ppermute | solution.py:485
  14.7 8.9 %collective-permute-start.8 = (bf16[128,512]{1,0:T(8,128)(2,1)S(1)}, bf16[128,512]{1,0:T(8,128)(2,1)S(1)}, u32[]{:S(2)}, u32[]{:S(2)}) collective-permute-start(bf16[128,512]{1,0:T(8,128)(2,1)S(1)} %add_convert_fusion), channel_id=1, source_target_pairs={{8,16},{12,20},{9,17},{13,21},{10,18},{14,22},{11,19},{15,23}} | collective-permute-start | bytes 393224 | tf_op jit(solution)/shard_map/ppermute | solution.py:457
  15.4 9.4 %collective-permute-start.13 = (bf16[512,256]{1,0:T(8,128)(2,1)S(1)}, bf16[512,256]{1,0:T(8,128)(2,1)S(1)}, u32[]{:S(2)}, u32[]{:S(2)}) collective-permute-start(bf16[512,256]{1,0:T(8,128)(2,1)S(1)} %get-tuple-element.24.refs_4_), channel_id=1, source_target_pairs={{0,8},{8,16},{16,24},{24,28},{28,20},{20,12},{12,4},{4,0},{1,9},{9... | collective-permute-start | bytes 786440 | tf_op jit(solution)/shard_map/ppermute | solution.py:485
  20.0 7.5 %collective-permute-start.21 = (bf16[512,256]{1,0:T(8,128)(2,1)S(1)}, bf16[512,256]{1,0:T(8,128)(2,1)S(1)}, u32[]{:S(2)}, u32[]{:S(2)}) collective-permute-start(bf16[512,256]{1,0:T(8,128)(2,1)S(1)} %get-tuple-element.26.refs_5_), channel_id=1, source_target_pairs={{0,8},{8,16},{16,24},{24,28},{28,20},{20,12},{12,4},{4,0},{1,9},{9... | collective-permute-start | bytes 786440 | tf_op jit(solution)/shard_map/ppermute | solution.py:485
  20.1 7.4 %collective-permute-start.17 = (bf16[512,256]{1,0:T(8,128)(2,1)S(1)}, bf16[512,256]{1,0:T(8,128)(2,1)S(1)}, u32[]{:S(2)}, u32[]{:S(2)}) collective-permute-start(bf16[512,256]{1,0:T(8,128)(2,1)S(1)} %get-tuple-element.26.refs_5_), channel_id=1, source_target_pairs={{8,0},{16,8},{24,16},{28,24},{20,28},{12,20},{4,12},{0,4},{9,1},{1... | collective-permute-start | bytes 786440 | tf_op jit(solution)/shard_map/ppermute | solution.py:485
  22.1 17.1 %collective-permute-start.1 = (bf16[512,512]{1,0:T(8,128)(2,1)S(1)}, bf16[512,512]{1,0:T(8,128)(2,1)S(1)}, u32[]{:S(2)}, u32[]{:S(2)}) collective-permute-start(bf16[512,512]{1,0:T(8,128)(2,1)S(1)} %get-tuple-element.21.refs_0_), channel_id=1, source_target_pairs={{0,2},{2,0},{1,3},{3,1},{4,6},{6,4},{5,7},{7,5},{8,10},{10,8},{9,1... | collective-permute-start | bytes 1572872 | tf_op jit(solution)/shard_map/ppermute | solution.py:22
  23.5 6.2 %collective-permute-start.9 = (bf16[128,512]{1,0:T(8,128)(2,1)S(1)}, bf16[128,512]{1,0:T(8,128)(2,1)S(1)}, u32[]{:S(2)}, u32[]{:S(2)}) collective-permute-start(bf16[128,512]{1,0:T(8,128)(2,1)S(1)} %collective-permute-done.8), channel_id=1, source_target_pairs={{16,24},{20,28},{17,25},{21,29},{18,26},{22,30},{19,27},{23,31}} | collective-permute-start | bytes 393224 | tf_op jit(solution)/shard_map/ppermute | solution.py:457
  24.7 12.1 %collective-permute-start.6 = (bf16[256,512]{1,0:T(8,128)(2,1)S(1)}, bf16[256,512]{1,0:T(8,128)(2,1)S(1)}, u32[]{:S(2)}, u32[]{:S(2)}) collective-permute-start(bf16[256,512]{1,0:T(8,128)(2,1)S(1)} %constant_dynamic-update-slice_fusion.refs_0_.refs_4_), channel_id=1, source_target_pairs={{0,2},{2,0},{1,3},{3,1},{4,6},{6,4},{5,7},{7,5},{8,10},{10,8},{9,1... | collective-permute-start | bytes 786440 | tf_op jit(solution)/shard_map/ppermute | solution.py:22
  27.5 9.6 %collective-permute-start.5 = (bf16[256,512]{1,0:T(8,128)(2,1)S(1)}, bf16[256,512]{1,0:T(8,128)(2,1)S(1)}, u32[]{:S(2)}, u32[]{:S(2)}) collective-permute-start(bf16[256,512]{1,0:T(8,128)(2,1)S(1)} %constant_dynamic-update-slice_fusion.refs_0_.refs_4_), channel_id=1, source_target_pairs={{0,1},{1,0},{2,3},{3,2},{4,5},{5,4},{6,7},{7,6},{8,9},{9,8},{10,11... | collective-permute-start | bytes 786440 | tf_op jit(solution)/shard_map/ppermute | solution.py:22
  27.5 11.7 %collective-permute-start.25 = (bf16[512,256]{1,0:T(8,128)(2,1)S(1)}, bf16[512,256]{1,0:T(8,128)(2,1)S(1)}, u32[]{:S(2)}, u32[]{:S(2)}) collective-permute-start(bf16[512,256]{1,0:T(8,128)(2,1)S(1)} %collective-permute-done.24.refs_8_), channel_id=1, source_target_pairs={{8,0},{16,8},{24,16},{28,24},{20,28},{12,20},{4,12},{0,4},{9,1},{1... | collective-permute-start | bytes 786440 | tf_op jit(solution)/shard_map/ppermute | solution.py:485
  29.8 18.9 %collective-permute-start = (bf16[512,512]{1,0:T(8,128)(2,1)S(1)}, bf16[512,512]{1,0:T(8,128)(2,1)S(1)}, u32[]{:S(2)}, u32[]{:S(2)}) collective-permute-start(bf16[512,512]{1,0:T(8,128)(2,1)S(1)} %get-tuple-element.21.refs_0_), channel_id=1, source_target_pairs={{0,1},{1,0},{2,3},{3,2},{4,5},{5,4},{6,7},{7,6},{8,9},{9,8},{10,11... | collective-permute-start | bytes 1572872 | tf_op jit(solution)/shard_map/ppermute | solution.py:22
  36.8 6.4 %collective-permute-start.14 = (bf16[512,256]{1,0:T(8,128)(2,1)S(1)}, bf16[512,256]{1,0:T(8,128)(2,1)S(1)}, u32[]{:S(2)}, u32[]{:S(2)}) collective-permute-start(bf16[512,256]{1,0:T(8,128)(2,1)S(1)} %collective-permute-done.13.refs_6_), channel_id=1, source_target_pairs={{0,8},{8,16},{16,24},{24,28},{28,20},{20,12},{12,4},{4,0},{1,9},{9... | collective-permute-start | bytes 786440 | tf_op jit(solution)/shard_map/ppermute | solution.py:485
  37.2 11.1 %collective-permute-start.22 = (bf16[512,256]{1,0:T(8,128)(2,1)S(1)}, bf16[512,256]{1,0:T(8,128)(2,1)S(1)}, u32[]{:S(2)}, u32[]{:S(2)}) collective-permute-start(bf16[512,256]{1,0:T(8,128)(2,1)S(1)} %collective-permute-done.21.refs_7_), channel_id=1, source_target_pairs={{0,8},{8,16},{16,24},{24,28},{28,20},{20,12},{12,4},{4,0},{1,9},{9... | collective-permute-start | bytes 786440 | tf_op jit(solution)/shard_map/ppermute | solution.py:485
  39.2 9.5 %collective-permute-start.18 = (bf16[512,256]{1,0:T(8,128)(2,1)S(1)}, bf16[512,256]{1,0:T(8,128)(2,1)S(1)}, u32[]{:S(2)}, u32[]{:S(2)}) collective-permute-start(bf16[512,256]{1,0:T(8,128)(2,1)S(1)} %collective-permute-done.17.refs_9_), channel_id=1, source_target_pairs={{8,0},{16,8},{24,16},{28,24},{20,28},{12,20},{4,12},{0,4},{9,1},{1... | collective-permute-start | bytes 786440 | tf_op jit(solution)/shard_map/ppermute | solution.py:485
  39.2 26.6 %collective-permute-start.2 = (bf16[512,512]{1,0:T(8,128)(2,1)S(1)}, bf16[512,512]{1,0:T(8,128)(2,1)S(1)}, u32[]{:S(2)}, u32[]{:S(2)}) collective-permute-start(bf16[512,512]{1,0:T(8,128)(2,1)S(1)} %collective-permute-done.1.refs_2_), channel_id=1, source_target_pairs={{0,1},{1,0},{2,3},{3,2},{4,5},{5,4},{6,7},{7,6},{8,9},{9,8},{10,11... | collective-permute-start | bytes 1572872 | tf_op jit(solution)/shard_map/ppermute | solution.py:22
  43.2 7.2 %collective-permute-start.11 = (bf16[128,512]{1,0:T(8,128)(2,1)S(1)}, bf16[128,512]{1,0:T(8,128)(2,1)S(1)}, u32[]{:S(2)}, u32[]{:S(2)}) collective-permute-start(bf16[128,512]{1,0:T(8,128)(2,1)S(1)} %add.11.refs_0_.refs_8_), channel_id=1, source_target_pairs={{0,2},{2,0},{1,3},{3,1},{4,6},{6,4},{5,7},{7,5},{8,10},{10,8},{9,1... | collective-permute-start | bytes 393224 | tf_op jit(solution)/shard_map/ppermute | solution.py:22
  48.3 6.9 %collective-permute-start.15 = (bf16[512,256]{1,0:T(8,128)(2,1)S(1)}, bf16[512,256]{1,0:T(8,128)(2,1)S(1)}, u32[]{:S(2)}, u32[]{:S(2)}) collective-permute-start(bf16[512,256]{1,0:T(8,128)(2,1)S(1)} %collective-permute-done.14.refs_4_.refs_10_), channel_id=1, source_target_pairs={{0,8},{8,16},{16,24},{24,28},{28,20},{20,12},{12,4},{4,0},{1,9},{9... | collective-permute-start | bytes 786440 | tf_op jit(solution)/shard_map/ppermute | solution.py:485
  48.7 1.8 %collective-permute-start.10 = (bf16[128,512]{1,0:T(8,128)(2,1)S(1)}, bf16[128,512]{1,0:T(8,128)(2,1)S(1)}, u32[]{:S(2)}, u32[]{:S(2)}) collective-permute-start(bf16[128,512]{1,0:T(8,128)(2,1)S(1)} %add.11.refs_0_.refs_8_), channel_id=1, source_target_pairs={{0,1},{1,0},{2,3},{3,2},{4,5},{5,4},{6,7},{7,6},{8,9},{9,8},{10,11... | collective-permute-start | bytes 393224 | tf_op jit(solution)/shard_map/ppermute | solution.py:22
  48.7 9.7 %collective-permute-start.19 = (bf16[512,256]{1,0:T(8,128)(2,1)S(1)}, bf16[512,256]{1,0:T(8,128)(2,1)S(1)}, u32[]{:S(2)}, u32[]{:S(2)}) collective-permute-start(bf16[512,256]{1,0:T(8,128)(2,1)S(1)} %collective-permute-done.18.refs_7_.refs_13_), channel_id=1, source_target_pairs={{8,0},{16,8},{24,16},{28,24},{20,28},{12,20},{4,12},{0,4},{9,1},{1... | collective-permute-start | bytes 786440 | tf_op jit(solution)/shard_map/ppermute | solution.py:485
  50.4 8.1 %collective-permute-start.7 = (bf16[256,512]{1,0:T(8,128)(2,1)S(1)}, bf16[256,512]{1,0:T(8,128)(2,1)S(1)}, u32[]{:S(2)}, u32[]{:S(2)}) collective-permute-start(bf16[256,512]{1,0:T(8,128)(2,1)S(1)} %collective-permute-done.6.refs_2_.refs_6_), channel_id=1, source_target_pairs={{0,1},{1,0},{2,3},{3,2},{4,5},{5,4},{6,7},{7,6},{8,9},{9,8},{10,11... | collective-permute-start | bytes 786440 | tf_op jit(solution)/shard_map/ppermute | solution.py:22
  50.5 13.3 %collective-permute-start.26 = (bf16[512,256]{1,0:T(8,128)(2,1)S(1)}, bf16[512,256]{1,0:T(8,128)(2,1)S(1)}, u32[]{:S(2)}, u32[]{:S(2)}) collective-permute-start(bf16[512,256]{1,0:T(8,128)(2,1)S(1)} %collective-permute-done.25.refs_6_.refs_12_), channel_id=1, source_target_pairs={{8,0},{16,8},{24,16},{28,24},{20,28},{12,20},{4,12},{0,4},{9,1},{1... | collective-permute-start | bytes 786440 | tf_op jit(solution)/shard_map/ppermute | solution.py:485
  55.1 18.6 %collective-permute-start.23 = (bf16[512,256]{1,0:T(8,128)(2,1)S(1)}, bf16[512,256]{1,0:T(8,128)(2,1)S(1)}, u32[]{:S(2)}, u32[]{:S(2)}) collective-permute-start(bf16[512,256]{1,0:T(8,128)(2,1)S(1)} %collective-permute-done.22.refs_5_.refs_11_), channel_id=1, source_target_pairs={{0,8},{8,16},{16,24},{24,28},{28,20},{20,12},{12,4},{4,0},{1,9},{9... | collective-permute-start | bytes 786440 | tf_op jit(solution)/shard_map/ppermute | solution.py:485
  58.4 6.2 %collective-permute-start.12 = (bf16[128,512]{1,0:T(8,128)(2,1)S(1)}, bf16[128,512]{1,0:T(8,128)(2,1)S(1)}, u32[]{:S(2)}, u32[]{:S(2)}) collective-permute-start(bf16[128,512]{1,0:T(8,128)(2,1)S(1)} %collective-permute-done.11.refs_2_.refs_10_), channel_id=1, source_target_pairs={{0,1},{1,0},{2,3},{3,2},{4,5},{5,4},{6,7},{7,6},{8,9},{9,8},{10,11... | collective-permute-start | bytes 393224 | tf_op jit(solution)/shard_map/ppermute | solution.py:22
  58.5 16.7 %collective-permute-start.27 = (bf16[256,256]{1,0:T(8,128)(2,1)S(1)}, bf16[256,256]{1,0:T(8,128)(2,1)S(1)}, u32[]{:S(2)}, u32[]{:S(2)}) collective-permute-start(bf16[256,256]{1,0:T(8,128)(2,1)S(1)} %get-tuple-element.33), channel_id=1, source_target_pairs={{0,8},{8,16},{16,24},{24,28},{28,20},{20,12},{12,4},{4,0},{1,9},{9... | collective-permute-start | bytes 393224 | tf_op jit(solution)/shard_map/ppermute | solution.py:485
  63.8 11.4 %collective-permute-start.28 = (bf16[256,256]{1,0:T(8,128)(2,1)S(1)}, bf16[256,256]{1,0:T(8,128)(2,1)S(1)}, u32[]{:S(2)}, u32[]{:S(2)}) collective-permute-start(bf16[256,256]{1,0:T(8,128)(2,1)S(1)} %get-tuple-element.34), channel_id=1, source_target_pairs={{8,0},{16,8},{24,16},{28,24},{20,28},{12,20},{4,12},{0,4},{9,1},{1... | collective-permute-start | bytes 393224 | tf_op jit(solution)/shard_map/ppermute | solution.py:485
  64.6 12.2 %collective-permute-start.16 = (bf16[256,256]{1,0:T(8,128)(2,1)S(1)}, bf16[256,256]{1,0:T(8,128)(2,1)S(1)}, u32[]{:S(2)}, u32[]{:S(2)}) collective-permute-start(bf16[256,256]{1,0:T(8,128)(2,1)S(1)} %get-tuple-element.25), channel_id=1, source_target_pairs={{0,8},{8,16},{16,24},{24,28},{28,20},{20,12},{12,4},{4,0},{1,9},{9... | collective-permute-start | bytes 393224 | tf_op jit(solution)/shard_map/ppermute | solution.py:485
  65.8 11.0 %collective-permute-start.20 = (bf16[256,256]{1,0:T(8,128)(2,1)S(1)}, bf16[256,256]{1,0:T(8,128)(2,1)S(1)}, u32[]{:S(2)}, u32[]{:S(2)}) collective-permute-start(bf16[256,256]{1,0:T(8,128)(2,1)S(1)} %get-tuple-element.27), channel_id=1, source_target_pairs={{8,0},{16,8},{24,16},{28,24},{20,28},{12,20},{4,12},{0,4},{9,1},{1... | collective-permute-start | bytes 393224 | tf_op jit(solution)/shard_map/ppermute | solution.py:485
  73.7 1.6 %copy-start = (f32[13,16,512]{2,1,0:T(8,128)S(1)}, f32[13,16,512]{2,1,0:T(8,128)}, u32[]{:S(2)}) copy-start(f32[13,16,512]{2,1,0:T(8,128)} %refs_18_.3) | copy-start | bytes 1277956
  73.7 1.6 %copy-start.1 = (bf16[512,128]{1,0:T(8,128)(2,1)S(1)}, bf16[512,128]{1,0:T(8,128)(2,1)}, u32[]{:S(2)}) copy-start(bf16[512,128]{1,0:T(8,128)(2,1)} %refs_17_.3) | copy-start | bytes 393220
